TPU v7x, 512 devices: a whole 4x8x8 slice. The times are simulated.
512 devices in a mesh: lvl: 8 (over y_hi, x), row: 64 (over z, y_lo, core).
Axes of the slice: x: 4, y: 8 (y_hi: 2, y_lo: 4; y = y_hi * 4 + y_lo), z: 8, core: 2. Of those that a mesh axis runs over, the one named last changes fastest.
Arguments:
- rhs: float32 [8, 64, 3, 128, 128], P('lvl', 'row'), may hold values from -6 to 6
- op_tiles: float32 [8, 64, 3, 7, 128, 128], P('lvl', 'row'), may hold values from -1 to 4
- op_cols: int32 [8, 64, 3, 7], P('lvl', 'row'), may hold values from 0 to 8, as said below
- link_tiles: float32 [8, 64, 3, 2, 128, 128], P('lvl', 'row'), may hold values from -0.3125 to 0.3125
- level_links: int32 [8, 64, 3, 2], P('lvl', 'row'), may hold values from 0 to 3, as said below
Outputs:
- levels: float32 [8, 64, 3, 128, 128], P('lvl', 'row')
Inputs may be any that keep to these rules, and one draw needn't show every extreme that they name: `op_cols`: tile 0 of each block row has code 3 + s (the block itself). Fine blocks have 7 distinct codes; every other block names only codes s, 3 + s, 6 + s of its own slot s. `level_links`: entries of blocks that are not fine are 0.
All inputs are finite; a program needn't handle non-finite values.
Results may differ from a plain program's by a relative error of at most 0.00021.
Values sent between devices are 32-bit elements; how exact they have to be, the bound alone decides.
A program may use at most 64 MiB of HBM per device.

v0:
```python
import jax
import jax.numpy as jnp
from jax import lax
from jax.sharding import PartitionSpec as P

CYCLES = 2


HIGH = lax.Precision.HIGHEST
COEF_ZERO = 0.9
COEF_ONE = -0.36
COEF_TWO = 0.05


def extended(block, sides, width):
    for axis, dim in sides:
        count = lax.axis_size(axis)
        forward = [(i, i + 1) for i in range(count - 1)]
        backward = [(target, source) for source, target in forward]
        low = lax.ppermute(
            lax.slice_in_dim(block, block.shape[dim] - width, None, axis=dim), axis, forward
        )
        high = lax.ppermute(lax.slice_in_dim(block, 0, width, axis=dim), axis, backward)
        block = jnp.concatenate([low, block, high], axis=dim)
    return block


def broadcast(block, axis, source):
    block = jnp.where(lax.axis_index(axis) == source, block, jnp.zeros_like(block))
    return lax.psum(block, axis)


def apply_operator(field, tiles, columns, keep):
    slots = field.shape[0]
    padded = extended(field[None], (("row", 0),), 1)
    candidates = padded.reshape((3 * slots,) + field.shape[1:])
    picked = candidates[columns]
    image = jnp.einsum("sjab,sjbn->san", tiles, picked, precision=HIGH)
    return image * keep[:, None, None]


def per_device(rhs, op_tiles, op_cols, link_tiles, level_links):
    n_lvl = lax.axis_size("lvl")
    fine_lvls = 5 * n_lvl // 8
    mid_lvls = max(n_lvl - fine_lvls - 1, 1)
    lvl_here = lax.axis_index("lvl")
    right = rhs[0, 0]
    tiles = op_tiles[0, 0]
    columns = op_cols[0, 0]
    links = link_tiles[0, 0]
    targets = level_links[0, 0]
    slots = right.shape[0]
    slot_ids = jnp.arange(slots)
    pair_ids = jnp.arange(2)
    is_fine = lvl_here < fine_lvls
    is_mid = (lvl_here >= fine_lvls) & (lvl_here < fine_lvls + mid_lvls)
    is_coarse = lvl_here == n_lvl - 1
    fine_keep = jnp.where(is_fine & (slot_ids >= 0), 1.0, 0.0).astype(jnp.float32)
    mid_keep = jnp.where(is_mid & ((slot_ids == 0) | (slot_ids == 2)), 1.0, 0.0).astype(jnp.float32)
    coarse_keep = jnp.where(is_coarse & (slot_ids == 1), 1.0, 0.0).astype(jnp.float32)
    all_keep = fine_keep + mid_keep + coarse_keep
    mid_flag = jnp.where(is_mid, 1.0, 0.0).astype(jnp.float32)
    place = (slot_ids[:, None] == 2 * pair_ids[None, :]).astype(jnp.float32) * mid_flag
    lvl_ids = jnp.arange(n_lvl)

    def lvl_table(target):
        by_lvl = (target[:, None] // 2 + fine_lvls == lvl_ids[None, :]).astype(jnp.float32)
        by_pair = (target[:, None] % 2 == pair_ids[None, :]).astype(jnp.float32)
        return by_lvl[:, :, None] * by_pair[:, None, :] * fine_keep[:, None, None]

    to_lvl = lvl_table(targets[:, 0])
    from_lvl = lvl_table(targets[:, 1])
    mid_restrict = jnp.stack([links[0, 0], links[2, 0]])
    mid_prolong = jnp.stack([links[0, 1], links[2, 1]])
    solution = jnp.zeros_like(right)
    mid_fix = jnp.zeros((2,) + right.shape[1:], jnp.float32)
    coarse_fix = jnp.zeros_like(right[0])
    for cycle in range(CYCLES):
        if cycle == 0:
            resid = right * fine_keep[:, None, None]
        else:
            resid = (right - apply_operator(solution, tiles, columns, all_keep)) * fine_keep[
                :, None, None
            ]
        terms = jnp.einsum("sab,sbn->san", links[:, 0], resid, precision=HIGH)
        dense = jnp.einsum("slm,san->lman", to_lvl, terms, precision=HIGH)
        mid_resid = lax.psum_scatter(dense, "lvl", scatter_dimension=0, tiled=True)[0] * mid_flag
        mid_part = jnp.einsum("mab,mbn->an", mid_restrict, mid_resid, precision=HIGH) * mid_flag
        fine_part = 0.5 * jnp.sum(terms * fine_keep[:, None, None], axis=0)
        coarse_resid = lax.psum(mid_part + fine_part, "lvl")
        level_resid = resid + jnp.einsum("sm,man->san", place, mid_resid, precision=HIGH)
        level_resid = level_resid + coarse_keep[:, None, None] * coarse_resid[None]
        first = apply_operator(level_resid, tiles, columns, all_keep)
        second = apply_operator(first, tiles, columns, all_keep)
        smooth = COEF_ZERO * level_resid + COEF_ONE * first + COEF_TWO * second
        coarse_fix = broadcast(smooth[1], "lvl", n_lvl - 1)
        mid_fix = jnp.stack([smooth[0], smooth[2]]) + jnp.einsum(
            "mab,bn->man", mid_prolong, coarse_fix, precision=HIGH
        )
        gathered = lax.all_gather(mid_fix[None], "lvl", axis=0, tiled=True)
        chosen = jnp.einsum("slm,lman->san", from_lvl, gathered, precision=HIGH)
        chosen = chosen + coarse_fix[None]
        fine_fix = smooth + jnp.einsum("sab,sbn->san", links[:, 1], chosen, precision=HIGH)
        solution = solution + fine_fix * fine_keep[:, None, None]
    levels = solution * fine_keep[:, None, None] + jnp.einsum(
        "sm,man->san", place, mid_fix, precision=HIGH
    )
    levels = levels + coarse_keep[:, None, None] * coarse_fix[None]
    return levels[None, None]


def solution(mesh):
    placed = (
        P("lvl", "row", None, None, None),
        P("lvl", "row", None, None, None, None),
        P("lvl", "row", None, None),
        P("lvl", "row", None, None, None, None),
        P("lvl", "row", None, None),
    )
    return jax.shard_map(
        per_device,
        mesh=mesh,
        in_specs=placed,
        out_specs=P("lvl", "row", None, None, None),
        check_vma=False,
    )
```

profile of v0, /device:TPU:8, one launch (start us, length us, event | category | flops | bytes accessed | tf_op | source)
XLA Modules:
  0.0 862.2 jit_solution(14442262137120643236)
XLA Ops:
  6.5 1.3 add_bitcast_fusion
  8.0 1.1 copy.25
  9.0 1.0 copy.77
  10.8 1.1 fusion.86
  11.9 1.2 copy.28
  14.1 1.5 slice_bitcast_fusion.7
  15.6 93.0 %reduce-scatter.3.cloned.1.call-done = f32[1,2,128,128]{3,2,1,0:T(8,128)} async-done(((f32[8,2,128,128]{3,2,1,0:T(8,128)}), f32[1,2,128,128]{3,2,1,0:T(8,128)}) %reduce-scatter.3.cloned.1.call-update) | async-done | bytes 131088 | tf_op jit(solution)/shard_map/reduce_scatter | solution.py:87
  108.6 1.8 fusion.78
  110.5 0.9 multiply_bitcast_fusion.1
  111.4 0.8 fusion.92
  112.4 107.7 %all-reduce.5.cloned.1.call-done = f32[128,128]{1,0:T(8,128)} async-done(((f32[128,128]{1,0:T(8,128)}), f32[128,128]{1,0:T(8,128)}) %all-reduce.5.cloned.1.call-update) | async-done | bytes 65552 | tf_op jit(solution)/shard_map/psum | solution.py:90
  220.1 0.9 copy.33
  221.1 1.9 collective-permute-start.1
  223.0 2.4 collective-permute-start
  226.2 3.8 collective-permute-done
  230.7 1.6 fusion.73
  232.3 1.9 collective-permute-start.3
  234.2 2.4 collective-permute-start.2
  237.4 3.8 collective-permute-done.2
  242.0 2.6 fusion.70
  245.3 115.5 %all-reduce.7.cloned.1.call-done = f32[128,128]{0,1:T(8,128)} async-done(((f32[128,128]{0,1:T(8,128)}), f32[128,128]{0,1:T(8,128)}) %all-reduce.7.cloned.1.call-update) | async-done | bytes 65552 | tf_op jit(solution)/shard_map/psum | solution.py:30
  360.8 1.2 convolution_add_fusion.1
  364.1 62.2 %all-gather.5.cloned.1.call-done = f32[16,128,128]{2,1,0:T(8,128)} async-done(((f32[2,128,128]{2,1,0:T(8,128)}), f32[16,128,128]{2,1,0:T(8,128)}) %all-gather.5.cloned.1.call-update) | async-done | bytes 1048592 | tf_op jit(solution)/shard_map/all_gather | solution.py:100
  426.3 2.5 fusion.82
  429.5 1.9 collective-permute-start.5
  431.4 2.6 collective-permute-start.4
  434.6 3.8 collective-permute-done.4
  439.1 1.5 fusion.58
  441.4 1.8 fusion.84
  443.2 1.2 copy.39
  444.5 88.9 %reduce-scatter.5.cloned.1.call-done = f32[1,2,128,128]{3,2,1,0:T(8,128)} async-done(((f32[8,2,128,128]{3,2,1,0:T(8,128)}), f32[1,2,128,128]{3,2,1,0:T(8,128)}) %reduce-scatter.5.cloned.1.call-update) | async-done | bytes 131088 | tf_op jit(solution)/shard_map/reduce_scatter | solution.py:87
  533.4 1.8 fusion.79
  535.3 0.9 multiply_bitcast_fusion
  537.2 107.5 %all-reduce.9.cloned.1.call-done = f32[128,128]{1,0:T(8,128)} async-done(((f32[128,128]{1,0:T(8,128)}), f32[128,128]{1,0:T(8,128)}) %all-reduce.9.cloned.1.call-update) | async-done | bytes 65552 | tf_op jit(solution)/shard_map/psum | solution.py:90
  644.7 0.9 copy.43
  645.8 1.9 collective-permute-start.7
  647.7 2.4 collective-permute-start.6
  650.9 3.8 collective-permute-done.6
  655.4 1.6 fusion.46
  656.9 1.9 collective-permute-start.9
  658.9 2.4 collective-permute-start.8
  662.0 3.8 collective-permute-done.8
  666.8 2.6 fusion.43
  670.2 115.5 %all-reduce.11.cloned.1.call-done = f32[128,128]{0,1:T(8,128)} async-done(((f32[128,128]{0,1:T(8,128)}), f32[128,128]{0,1:T(8,128)}) %all-reduce.11.cloned.1.call-update) | async-done | bytes 65552 | tf_op jit(solution)/shard_map/psum | solution.py:30
  785.7 1.1 convolution_add_fusion
  788.7 62.7 %all-gather.7.cloned.1.call-done = f32[16,128,128]{2,1,0:T(8,128)} async-done(((f32[2,128,128]{2,1,0:T(8,128)}), f32[16,128,128]{2,1,0:T(8,128)}) %all-gather.7.cloned.1.call-update) | async-done | bytes 1048592 | tf_op jit(solution)/shard_map/all_gather | solution.py:100
  851.3 2.5 fusion.80
  854.6 0.8 copy.49
  (134 shorter events, 17.8 us)
Async XLA Ops:
  6.5 224.2 %copy-start = (f32[1,1,3,7,128,128]{5,4,3,2,1,0:T(8,128)S(1)}, f32[1,1,3,7,128,128]{5,4,3,2,1,0:T(8,128)}, u32[]{:S(2)}) copy-start(f32[1,1,3,7,128,128]{5,4,3,2,1,0:T(8,128)} %param.6) | copy-start | bytes 4128772
  6.5 102.1 %reduce-scatter.3.cloned.1.call-start = ((), (), s32[]{:S(2)}) async-start(), calls=%async_computation.2 | async-start | bytes 1179648 | tf_op jit(solution)/shard_map/reduce_scatter | solution.py:87
  7.9 4.0 copy-start.30
  13.1 207.0 %all-reduce.5.cloned.1.call-start = ((), (), s32[]{:S(2)}) async-start(), calls=%async_computation.3 | async-start | bytes 131072 | tf_op jit(solution)/shard_map/psum | solution.py:90
  13.4 207.7 %copy-start.27 = (s32[2]{0:T(128)}, s32[2]{0:T(128)S(1)}, u32[]{:S(2)}) copy-start(s32[2]{0:T(128)S(1)} %iota_multiply_fusion) | copy-start | bytes 28
  13.4 228.5 %copy-start.25 = (f32[3]{0:T(128)}, f32[3]{0:T(128)S(1)}, u32[]{:S(2)}) copy-start(f32[3]{0:T(128)S(1)} %and_select_fusion.3) | copy-start | bytes 40
  14.1 96.4 %copy-start.19 = (f32[1,128,128]{2,1,0:T(8,128)}, f32[1,128,128]{2,1,0:T(8,128)S(1)}, u32[]{:S(2)}) copy-start(f32[1,128,128]{2,1,0:T(8,128)S(1)} %get-tuple-element.12) | copy-start | bytes 196612
  15.6 95.8 %copy-start.21 = (f32[1,128,128]{2,1,0:T(8,128)}, f32[1,128,128]{2,1,0:T(8,128)S(1)}, u32[]{:S(2)}) copy-start(f32[1,128,128]{2,1,0:T(8,128)S(1)} %get-tuple-element.10) | copy-start | bytes 196612
  110.5 250.3 %all-reduce.7.cloned.1.call-start = ((), (), s32[]{:S(2)}) async-start(), calls=%async_computation.4 | async-start | bytes 131072 | tf_op jit(solution)/shard_map/psum | solution.py:30
  112.3 113.9 %copy-start.8 = (f32[3,128,128]{1,2,0:T(8,128)}, f32[3,128,128]{1,2,0:T(8,128)S(1)}, u32[]{:S(2)}) copy-start(f32[3,128,128]{1,2,0:T(8,128)S(1)} %copy.30) | copy-start | bytes 589828
  221.0 5.2 copy-start.15
  221.1 5.1 collective-permute-start.1
  223.0 7.0 collective-permute-start
  232.3 9.0 %copy-start.7 = (f32[3,128,128]{2,1,0:T(8,128)}, f32[3,128,128]{2,1,0:T(8,128)S(1)}, u32[]{:S(2)}) copy-start(f32[3,128,128]{2,1,0:T(8,128)S(1)} %fusion.73) | copy-start | bytes 589828
  232.3 5.1 collective-permute-start.3
  234.2 7.0 collective-permute-start.2
  245.2 183.8 %copy-start.2 = (f32[1,1,3,2,128,128]{5,4,2,3,1,0:T(8,128)S(1)}, f32[1,1,3,2,128,128]{5,4,2,3,1,0:T(8,128)}, u32[]{:S(2)}) copy-start(f32[1,1,3,2,128,128]{5,4,2,3,1,0:T(8,128)} %copy-done.1) | copy-start | bytes 1179652
  245.2 181.1 %all-gather.5.cloned.1.call-start = ((), (), s32[]{:S(2)}) async-start(), calls=%async_computation.8 | async-start | bytes 1179648 | tf_op jit(solution)/shard_map/all_gather | solution.py:100
  360.8 68.2 %copy-start.24 = (f32[128,128]{0,1:T(8,128)S(1)}, f32[128,128]{0,1:T(8,128)}, u32[]{:S(2)}) copy-start(f32[128,128]{0,1:T(8,128)} %all-reduce.7.cloned.1.call-done) | copy-start | bytes 196612
  362.8 170.6 %reduce-scatter.5.cloned.1.call-start = ((), (), s32[]{:S(2)}) async-start(), calls=%async_computation.5 | async-start | bytes 1179648 | tf_op jit(solution)/shard_map/reduce_scatter | solution.py:87
  363.5 62.8 %copy-start.31 = (f32[3,2]{0,1:T(2,128)}, f32[3,2]{0,1:T(2,128)S(1)}, u32[]{:S(2)}) copy-start(f32[3,2]{0,1:T(2,128)S(1)} %compare_convert_fusion) | copy-start | bytes 76
  429.5 9.0 %copy-start.9 = (f32[3,128,128]{1,2,0:T(8,128)}, f32[3,128,128]{1,2,0:T(8,128)S(1)}, u32[]{:S(2)}) copy-start(f32[3,128,128]{1,2,0:T(8,128)S(1)} %fusion.30) | copy-start | bytes 589828
  429.5 5.1 collective-permute-start.5
  431.4 7.0 collective-permute-start.4
  440.7 204.9 %copy-start.5 = (f32[3,128,128]{1,2,0:T(8,128)}, f32[3,128,128]{1,2,0:T(8,128)S(1)}, u32[]{:S(2)}) copy-start(f32[3,128,128]{1,2,0:T(8,128)S(1)} %fusion.58) | copy-start | bytes 589828
  443.2 90.3 %copy-start.20 = (f32[1,128,128]{2,1,0:T(8,128)S(1)}, f32[1,128,128]{2,1,0:T(8,128)}, u32[]{:S(2)}) copy-start(f32[1,128,128]{2,1,0:T(8,128)} %copy-done.19) | copy-start | bytes 196612
  443.2 90.3 %copy-start.22 = (f32[1,128,128]{2,1,0:T(8,128)S(1)}, f32[1,128,128]{2,1,0:T(8,128)}, u32[]{:S(2)}) copy-start(f32[1,128,128]{2,1,0:T(8,128)} %copy-done.21) | copy-start | bytes 196612
  444.4 91.9 %copy-start.28 = (s32[2]{0:T(128)S(1)}, s32[2]{0:T(128)}, u32[]{:S(2)}) copy-start(s32[2]{0:T(128)} %copy-done.27) | copy-start | bytes 28
  444.4 201.3 %copy-start.26 = (f32[3]{0:T(128)S(1)}, f32[3]{0:T(128)}, u32[]{:S(2)}) copy-start(f32[3]{0:T(128)} %copy-done.25) | copy-start | bytes 40
  444.4 200.3 %all-reduce.9.cloned.1.call-start = ((), (), s32[]{:S(2)}) async-start(), calls=%async_computation.6 | async-start | bytes 131072 | tf_op jit(solution)/shard_map/psum | solution.py:90
  535.3 250.4 %all-reduce.11.cloned.1.call-start = ((), (), s32[]{:S(2)}) async-start(), calls=%async_computation.7 | async-start | bytes 131072 | tf_op jit(solution)/shard_map/psum | solution.py:30
  537.1 113.7 %copy-start.12 = (f32[3,128,128]{1,2,0:T(8,128)}, f32[3,128,128]{1,2,0:T(8,128)S(1)}, u32[]{:S(2)}) copy-start(f32[3,128,128]{1,2,0:T(8,128)S(1)} %copy.41) | copy-start | bytes 589828
  645.7 5.2 copy-start.16
  645.8 5.1 collective-permute-start.7
  647.7 7.0 collective-permute-start.6
  656.9 9.0 %copy-start.11 = (f32[3,128,128]{2,1,0:T(8,128)}, f32[3,128,128]{2,1,0:T(8,128)S(1)}, u32[]{:S(2)}) copy-start(f32[3,128,128]{2,1,0:T(8,128)S(1)} %fusion.46) | copy-start | bytes 589828
  656.9 5.1 collective-permute-start.9
  658.9 7.0 collective-permute-start.8
  666.8 118.8 %copy-start.17 = (f32[1,128,128]{2,1,0:T(8,128)S(1)}, f32[1,128,128]{2,1,0:T(8,128)}, u32[]{:S(2)}) copy-start(f32[1,128,128]{2,1,0:T(8,128)} %get-tuple-element.11) | copy-start | bytes 196612
  666.8 118.8 %copy-start.18 = (f32[1,128,128]{2,1,0:T(8,128)S(1)}, f32[1,128,128]{2,1,0:T(8,128)}, u32[]{:S(2)}) copy-start(f32[1,128,128]{2,1,0:T(8,128)} %get-tuple-element.9) | copy-start | bytes 196612
  669.5 118.1 %copy-start.13 = (f32[3,128,128]{1,2,0:T(8,128)}, f32[3,128,128]{1,2,0:T(8,128)S(1)}, u32[]{:S(2)}) copy-start(f32[3,128,128]{1,2,0:T(8,128)S(1)} %fusion.43) | copy-start | bytes 589828
  669.5 118.2 %copy-start.29 = (s32[2]{0:T(128)S(1)}, s32[2]{0:T(128)}, u32[]{:S(2)}) copy-start(s32[2]{0:T(128)} %copy-done.27) | copy-start | bytes 28
  669.5 181.8 %copy-start.32 = (f32[3,2]{0,1:T(2,128)S(1)}, f32[3,2]{0,1:T(2,128)}, u32[]{:S(2)}) copy-start(f32[3,2]{0,1:T(2,128)} %copy-done.31) | copy-start | bytes 76
  670.2 181.2 %all-gather.7.cloned.1.call-start = ((), (), s32[]{:S(2)}) async-start(), calls=%async_computation.9 | async-start | bytes 1179648 | tf_op jit(solution)/shard_map/all_gather | solution.py:100
  787.7 66.3 %copy-start.4 = (f32[1,1,3,2,128,128]{5,4,2,3,1,0:T(8,128)S(1)}, f32[1,1,3,2,128,128]{5,4,2,3,1,0:T(8,128)}, u32[]{:S(2)}) copy-start(f32[1,1,3,2,128,128]{5,4,2,3,1,0:T(8,128)} %copy-done.1) | copy-start | bytes 1179652
  787.7 66.3 %copy-start.10 = (f32[3,128,128]{1,2,0:T(8,128)S(1)}, f32[3,128,128]{1,2,0:T(8,128)}, u32[]{:S(2)}) copy-start(f32[3,128,128]{1,2,0:T(8,128)} %copy-done.9) | copy-start | bytes 589828
  787.7 66.3 %copy-start.14 = (f32[3,128,128]{1,2,0:T(8,128)S(1)}, f32[3,128,128]{1,2,0:T(8,128)}, u32[]{:S(2)}) copy-start(f32[3,128,128]{1,2,0:T(8,128)} %copy-done.13) | copy-start | bytes 589828
  787.7 66.3 %copy-start.23 = (f32[128,128]{0,1:T(8,128)S(1)}, f32[128,128]{0,1:T(8,128)}, u32[]{:S(2)}) copy-start(f32[128,128]{0,1:T(8,128)} %all-reduce.11.cloned.1.call-done) | copy-start | bytes 196612
  (4 other events, 7.1 us)
Sparse Core Ops, SparseCore 0:
  13.2 95.3 reduce-scatter.2
  111.5 108.5 all-reduce.4
  245.3 115.4 all-reduce.6
  363.8 62.3 all-gather.4
  444.5 88.8 reduce-scatter.4
  536.2 108.4 all-reduce.8
  670.3 115.3 all-reduce.10
  788.9 62.3 all-gather.6
where the time goes:
time: 863 us; the launch traced here: 862 us
  waiting for transfers between devices  776 us (90%)
  matrix products  28.1 us (3%)
  starting transfers between devices  22.1 us (3%)
  local copies, waits for them, and re-layouts  15.7 us (2%)
  between operations  14.3 us (2%)
    psum x2, waiting for transfers between devices, broadcast(): return lax.psum(block, axis)  231 us
    psum x2, waiting for transfers between devices, per_device(): coarse_resid = lax.psum(mid_part + fine_part, 'lvl')  215 us
    reduce_scatter x2, waiting for transfers between devices, per_device(): lax.psum_scatter(dense, 'lvl', scatter_dimension=0, tiled=True)[0]  182 us
    all_gather x2, waiting for transfers between devices, per_device(): gathered = lax.all_gather(mid_fix[None], 'lvl', axis=0, tiled=True)  125 us
    ppermute x5, waiting for transfers between devices, extended(): lax.ppermute(lax.slice_in_dim(block, block.shape[dim] - width, None, axis...  19.1 us
  transfers between devices with their start and end apart: 18, of which 18 were waited for; matrix products, arithmetic and copies ran while one was open for 1% of the time, Pallas kernels for 0%

commit v1 on v0

v1 whole, which is shorter than its diff:
```python
import jax
import jax.numpy as jnp
from jax import lax
from jax.experimental import pallas as pl
from jax.experimental.pallas import tpu as pltpu
from jax.sharding import PartitionSpec as P

CYCLES = 2
B = 128
SLOTS = 3
OPT = 7
COEF_ZERO = 0.9
COEF_ONE = -0.36
COEF_TWO = 0.05
MESH = pl.DeviceIdType.MESH
F32 = jnp.float32
BF16 = jnp.bfloat16


def halves(value):
    high = value.astype(BF16)
    return high, (value - high.astype(F32)).astype(BF16)


def stacked(value):
    return jnp.concatenate(halves(value), axis=0)


def beside(value):
    return jnp.concatenate(halves(value), axis=1)


def product(left, right):
    full = jnp.dot(left, right, preferred_element_type=F32)
    rows, columns = full.shape[0] // 2, full.shape[1] // 2
    cross = full[:rows, columns:] + full[rows:, :columns]
    return full[:rows, :columns] + (cross + full[rows:, columns:])


def kernel(
    n_row,
    rhs_hbm, ops_hbm, cols, links_hbm, targets, out,
    rhs, ops, links, wide, small, link_parts,
    field, halo, rs_src, rs_in, sum_src, mid_in, part_src, coarse_in, fix, fbuf,
    sol, smooth,
    in_sem, halo_send, halo_recv, rs_send, rs_recv, sum_send, mid_recv, four_send,
    part_send, coarse_recv, fix_send, fix_recv, f_send, gather_send, f_recv,
):
    lvl = lax.axis_index("lvl")
    row = lax.axis_index("row")
    is_fine = lvl < 5
    is_mid = (lvl >= 5) & (lvl < 7)
    is_coarse = lvl == 7
    has = (row > 0, row < n_row - 1)
    near = (row - 1, row + 1)

    loads = [
        pltpu.make_async_copy(rhs_hbm, rhs, in_sem.at[0]),
        pltpu.make_async_copy(links_hbm, links, in_sem.at[1]),
        pltpu.make_async_copy(ops_hbm, ops, in_sem.at[2]),
    ]
    for load in loads:
        load.start()

    barrier = pltpu.get_barrier_semaphore()
    for step in range(1, 8):
        pl.semaphore_signal(
            barrier, inc=1, device_id={"lvl": lax.rem(lvl + step, 8), "row": row}, device_id_type=MESH
        )
    for side in range(2):
        @pl.when(has[side])
        def _():
            pl.semaphore_signal(
                barrier, inc=1, device_id={"lvl": lvl, "row": near[side]}, device_id_type=MESH
            )

    def meet():
        pl.semaphore_wait(barrier, 7 + sum(one.astype(jnp.int32) for one in has))

    def copy(src, dst, send, recv, to_lvl, to_row=None):
        return pltpu.make_async_remote_copy(
            src_ref=src, dst_ref=dst, send_sem=send, recv_sem=recv,
            device_id={"lvl": to_lvl, "row": row if to_row is None else to_row},
            device_id_type=MESH,
        )

    def halo_copy(turn, side, src, rows):
        other = 1 - side
        return copy(
            src.at[pl.ds(0, rows)], halo.at[turn, other, pl.ds(0, rows)],
            halo_send.at[turn, side], halo_recv.at[turn, other], lvl, near[side],
        )

    def halo_start(turn, src, rows):
        for side in range(2):
            @pl.when(has[side])
            def _():
                halo_copy(turn, side, src, rows).start()

    def halo_sent(turn, src, rows):
        for side in range(2):
            @pl.when(has[side])
            def _():
                halo_copy(turn, side, src, rows).wait_send()

    def halo_arrived(turn, side, rows):
        pltpu.make_async_copy(
            halo.at[turn, side, pl.ds(0, rows)], halo.at[turn, side, pl.ds(0, rows)],
            halo_recv.at[turn, side],
        ).wait()

    def arrived(ref, sem):
        pltpu.make_async_copy(ref, ref, sem).wait()

    def split_links():
        loads[1].wait()
        for s in range(SLOTS):
            for kind in range(2):
                link_parts[s, kind] = stacked(links[s, kind])

    def code_of(s, j):
        return cols[s * OPT + j]

    def gathered_tile(s, code):
        total = jnp.zeros((B, B), F32)
        for j in range(OPT):
            total = total + jnp.where(code_of(s, j) == code, F32(1), F32(0)) * ops[s * OPT + j]
        return total

    @pl.when(is_fine)
    def _():
        split_links()
        loads[0].wait()

        def restrict(cycle, resid_of):
            terms = [
                product(link_parts[s, 0], beside(resid_of(s))) for s in range(SLOTS)
            ]
            for k in range(4):
                total = jnp.zeros((B, B), F32)
                for s in range(SLOTS):
                    hit = jnp.where(targets[s * 2] == k, F32(1), F32(0))
                    total = total + hit * terms[s]
                rs_src[cycle, k] = total

        def rs_copy(cycle, step):
            to = lax.rem(lvl + step, 4)
            return copy(
                rs_src.at[cycle, to], rs_in.at[cycle, lvl],
                rs_send.at[cycle, step], rs_recv.at[cycle, lvl], to,
            )

        def sum_copy(cycle):
            return copy(
                sum_src.at[cycle], mid_in.at[cycle, lax.rem(lvl, 2), 0],
                sum_send.at[cycle], mid_recv.at[cycle, lax.rem(lvl, 2), 0], 5 + lvl // 2,
            )

        def four_copy(cycle, k):
            return copy(
                rs_src.at[cycle, k], mid_in.at[cycle, k % 2, 1],
                four_send.at[cycle, k], mid_recv.at[cycle, k % 2, 1], 5 + k // 2,
            )

        def gather_copy(cycle, step):
            return copy(
                fbuf.at[cycle, lvl], fbuf.at[cycle, lvl],
                gather_send.at[cycle, step], f_recv.at[cycle, lvl], lax.rem(lvl + step, 4),
            )

        def send_terms(cycle):
            @pl.when(lvl < 4)
            def _():
                for step in range(1, 4):
                    rs_copy(cycle, step).start()

            @pl.when(lvl == 4)
            def _():
                for k in range(4):
                    four_copy(cycle, k).start()

        def send_sum(cycle):
            @pl.when(lvl < 4)
            def _():
                total = rs_src[cycle, lvl]
                for step in range(1, 4):
                    source = lax.rem(lvl + step, 4)
                    arrived(rs_in.at[cycle, source], rs_recv.at[cycle, source])
                    total = total + rs_in[cycle, source]
                sum_src[cycle] = total
                sum_copy(cycle).start()

        def collect(cycle):
            @pl.when(lvl < 4)
            def _():
                arrived(fbuf.at[cycle, lvl], f_recv.at[cycle, lvl])
                for step in range(1, 4):
                    gather_copy(cycle, step).start()
                for step in range(1, 4):
                    source = lax.rem(lvl + step, 4)
                    arrived(fbuf.at[cycle, source], f_recv.at[cycle, source])

            @pl.when(lvl == 4)
            def _():
                for k in range(4):
                    arrived(fbuf.at[cycle, k], f_recv.at[cycle, k])

        def image(turn, src, dst):
            dst[...] = product(wide[1], beside(src[...]))
            for side in range(2):
                @pl.when(has[side])
                def _():
                    halo_arrived(turn, side, SLOTS * B)
                    dst[...] = dst[...] + product(wide[2 * side], beside(halo[turn, side]))

        restrict(0, lambda s: rhs[pl.ds(s * B, B)])
        meet()
        send_terms(0)
        halo_start(0, rhs, SLOTS * B)

        loads[2].wait()

        def dense(s, carry):
            for code in range(3 * SLOTS):
                high, low = halves(gathered_tile(s, code))
                columns = pl.ds((code % SLOTS) * B, B)
                wide[code // SLOTS, pl.ds(pl.multiple_of(s * B, B), B), columns] = high
                wide[code // SLOTS, pl.ds(pl.multiple_of((SLOTS + s) * B, B), B), columns] = low
            return carry

        lax.fori_loop(0, SLOTS, dense, 0)

        sent = []
        for cycle in range(CYCLES):
            if cycle == 0:
                base = 0
                resid = rhs
                sent.append((0, rhs))
            else:
                base = 3
                halo_start(2, sol, SLOTS * B)
                image(2, sol, smooth)
                resid = field.at[3]
                resid[...] = rhs[...] - smooth[...]
                restrict(1, lambda s: field[3, pl.ds(s * B, B)])
                send_terms(1)
                halo_start(3, resid, SLOTS * B)
                sent.append((2, sol))
                sent.append((3, resid))
            send_sum(cycle)
            first = field.at[base + 1]
            image(base, resid, first)

            @pl.when(lvl < 4)
            def _():
                sum_copy(cycle).wait_send()

            halo_start(base + 1, first, SLOTS * B)
            sent.append((base + 1, first))
            image(base + 1, first, smooth)
            smooth[...] = COEF_ZERO * resid[...] + COEF_ONE * first[...] + COEF_TWO * smooth[...]
            if cycle == 1:
                smooth[...] = sol[...] + smooth[...]
            collect(cycle)
            dest = sol if cycle == 0 else out
            for s in range(SLOTS):
                chosen = fbuf[cycle, targets[s * 2 + 1]]
                rows = pl.ds(s * B, B)
                dest[rows] = smooth[rows] + product(link_parts[s, 1], beside(chosen))

        for turn, src in sent:
            halo_sent(turn, src, SLOTS * B)
        for cycle in range(CYCLES):
            @pl.when(lvl < 4)
            def _():
                for step in range(1, 4):
                    rs_copy(cycle, step).wait_send()
                    gather_copy(cycle, step).wait_send()

            @pl.when(lvl == 4)
            def _():
                for k in range(4):
                    four_copy(cycle, k).wait_send()

    def narrow(p, s):
        for near_row in range(3):
            small[p, near_row] = stacked(gathered_tile(s, near_row * SLOTS + s))

    def level_image(turn, count, dst):
        rows = count * B
        for p in range(count):
            part = pl.ds(p * B, B)
            dst[part] = product(small[p, 1], beside(field[turn, part]))
        for side in range(2):
            @pl.when(has[side])
            def _():
                halo_arrived(turn, side, rows)
                for p in range(count):
                    part = pl.ds(p * B, B)
                    dst[part] = dst[part] + product(small[p, 2 * side], beside(halo[turn, side, part]))

    def level_smooth(base, count):
        rows = count * B
        first = field.at[base + 1]
        level_image(base, count, first)
        halo_start(base + 1, first, rows)
        level_image(base + 1, count, smooth)
        part = pl.ds(0, rows)
        smooth[part] = (
            COEF_ZERO * field[base, part] + COEF_ONE * first[part] + COEF_TWO * smooth[part]
        )

    @pl.when(is_mid)
    def _():
        pair = lvl - 5
        split_links()
        eye = (
            lax.broadcasted_iota(jnp.int32, (B, B), 0) == lax.broadcasted_iota(jnp.int32, (B, B), 1)
        ).astype(F32)
        for p in range(2):
            link_parts[2 * p, 0] = stacked(links[2 * p, 0] + 0.5 * eye)
        loads[0].wait()
        loads[2].wait()
        for p in range(2):
            narrow(p, 2 * p)
        meet()

        def part_copy(cycle):
            return copy(
                part_src.at[cycle], coarse_in.at[cycle, pair],
                part_send.at[cycle], coarse_recv.at[cycle, pair], 7,
            )

        def f_copy(cycle, p, four):
            k = 2 * pair + p
            return copy(
                fbuf.at[cycle, k], fbuf.at[cycle, k],
                f_send.at[cycle, p, four], f_recv.at[cycle, k], 4 if four else k,
            )

        for cycle in range(CYCLES):
            base = 3 * cycle
            for p in range(2):
                for source in (1, 0):
                    arrived(mid_in.at[cycle, p, source], mid_recv.at[cycle, p, source])
                field[base, pl.ds(p * B, B)] = mid_in[cycle, p, 0] + mid_in[cycle, p, 1]
            total = product(link_parts[0, 0], beside(field[base, pl.ds(0, B)]))
            part_src[cycle] = total + product(link_parts[2, 0], beside(field[base, pl.ds(B, B)]))
            part_copy(cycle).start()
            halo_start(base, field.at[base], 2 * B)
            level_smooth(base, 2)
            arrived(fix.at[cycle], fix_recv.at[cycle])
            coarse = beside(fix[cycle])
            for p in range(2):
                value = smooth[pl.ds(p * B, B)] + product(link_parts[2 * p, 1], coarse)
                smooth[pl.ds(p * B, B)] = value
                fbuf[cycle, 2 * pair + p] = value + fix[cycle]
                for four in range(2):
                    f_copy(cycle, p, four).start()
        out[pl.ds(0, B)] = smooth[pl.ds(0, B)]
        out[pl.ds(B, B)] = jnp.zeros((B, B), F32)
        out[pl.ds(2 * B, B)] = smooth[pl.ds(B, B)]
        for cycle in range(CYCLES):
            part_copy(cycle).wait_send()
            for turn in (3 * cycle, 3 * cycle + 1):
                halo_sent(turn, field.at[turn], 2 * B)
            for p in range(2):
                for four in range(2):
                    f_copy(cycle, p, four).wait_send()

    @pl.when(is_coarse)
    def _():
        loads[0].wait()
        loads[1].wait()
        loads[2].wait()
        narrow(0, 1)
        meet()

        def fix_copy(cycle, pair):
            return copy(
                fix.at[cycle], fix.at[cycle], fix_send.at[cycle, pair], fix_recv.at[cycle], 5 + pair
            )

        for cycle in range(CYCLES):
            base = 3 * cycle
            for pair in range(2):
                arrived(coarse_in.at[cycle, pair], coarse_recv.at[cycle, pair])
            field[base, pl.ds(0, B)] = coarse_in[cycle, 0] + coarse_in[cycle, 1]
            halo_start(base, field.at[base], B)
            level_smooth(base, 1)
            fix[cycle] = smooth[pl.ds(0, B)]
            for pair in range(2):
                fix_copy(cycle, pair).start()
        out[pl.ds(0, B)] = jnp.zeros((B, B), F32)
        out[pl.ds(B, B)] = fix[CYCLES - 1]
        out[pl.ds(2 * B, B)] = jnp.zeros((B, B), F32)
        for cycle in range(CYCLES):
            for turn in (3 * cycle, 3 * cycle + 1):
                halo_sent(turn, field.at[turn], B)
            for pair in range(2):
                fix_copy(cycle, pair).wait_send()


def solution(mesh):
    n_row = mesh.shape["row"]

    def per_device(rhs, op_tiles, op_cols, link_tiles, level_links):
        dma = pltpu.SemaphoreType.DMA
        block = lambda *lead: pltpu.VMEM(lead + (B, B), F32)
        out = pl.pallas_call(
            lambda *refs: kernel(n_row, *refs),
            name="multigrid",
            out_shape=jax.ShapeDtypeStruct((SLOTS * B, B), F32),
            in_specs=[
                pl.BlockSpec(memory_space=pl.ANY),
                pl.BlockSpec(memory_space=pl.ANY),
                pl.BlockSpec(memory_space=pltpu.SMEM),
                pl.BlockSpec(memory_space=pl.ANY),
                pl.BlockSpec(memory_space=pltpu.SMEM),
            ],
            out_specs=pl.BlockSpec(memory_space=pltpu.VMEM),
            scratch_shapes=[
                pltpu.VMEM((SLOTS * B, B), F32),
                block(SLOTS * OPT),
                block(SLOTS, 2),
                pltpu.VMEM((3, 2 * SLOTS * B, SLOTS * B), BF16),
                pltpu.VMEM((2, 3, 2 * B, B), BF16),
                pltpu.VMEM((SLOTS, 2, 2 * B, B), BF16),
                pltpu.VMEM((5, SLOTS * B, B), F32),
                pltpu.VMEM((5, 2, SLOTS * B, B), F32),
                block(CYCLES, 4),
                block(CYCLES, 4),
                block(CYCLES),
                block(CYCLES, 2, 2),
                block(CYCLES),
                block(CYCLES, 2),
                block(CYCLES),
                block(CYCLES, 4),
                pltpu.VMEM((SLOTS * B, B), F32),
                pltpu.VMEM((SLOTS * B, B), F32),
                dma((3,)),
                dma((5, 2)),
                dma((5, 2)),
                dma((CYCLES, 4)),
                dma((CYCLES, 4)),
                dma((CYCLES,)),
                dma((CYCLES, 2, 2)),
                dma((CYCLES, 4)),
                dma((CYCLES,)),
                dma((CYCLES, 2)),
                dma((CYCLES, 2)),
                dma((CYCLES,)),
                dma((CYCLES, 2, 2)),
                dma((CYCLES, 4)),
                dma((CYCLES, 4)),
            ],
            compiler_params=pltpu.CompilerParams(
                collective_id=0, has_side_effects=True, vmem_limit_bytes=60 * 1024 * 1024
            ),
        )(
            rhs.reshape(SLOTS * B, B),
            op_tiles.reshape(SLOTS * OPT, B, B),
            op_cols.reshape(SLOTS * OPT),
            link_tiles.reshape(SLOTS, 2, B, B),
            level_links.reshape(SLOTS * 2),
        )
        return out.reshape(1, 1, SLOTS, B, B)

    placed = (
        P("lvl", "row", None, None, None),
        P("lvl", "row", None, None, None, None),
        P("lvl", "row", None, None),
        P("lvl", "row", None, None, None, None),
        P("lvl", "row", None, None),
    )
    return jax.shard_map(
        per_device,
        mesh=mesh,
        in_specs=placed,
        out_specs=P("lvl", "row", None, None, None),
        check_vma=False,
    )
```

time: 863 us -> 99.2 us (0.11)
  the two profiles are of different devices: /device:TPU:8 before, /device:TPU:217 now
where the time goes in v1:
time: 99.2 us; the launch traced here: 99 us
  Pallas kernels  94.6 us (95%)
  local copies, waits for them, and re-layouts  3.63 us (4%)
    pallas_call x1, Pallas kernels, per_device(): pl.pallas_call(lambda *refs: kernel(n_row, *refs), name='multigrid', out_...  94.6 us
    unnamed x2, local copies, waits for them, and re-layouts  2.38 us

profile of v1, /device:TPU:217, one launch (start us, length us, event | category | flops | bytes accessed | tf_op | source)
XLA Modules:
  0.0 99.0 jit_solution(18118116342506714354)
XLA Ops:
  0.0 0.7 reduce
  0.7 0.6 reshape.20.refs_2_
  1.3 0.8 copy.7
  2.1 0.7 reshape.22.refs_4_
  2.7 94.6 %multigrid.1 = f32[384,128]{1,0:T(8,128)} custom-call(f32[384,128]{1,0:T(8,128)} %bitcast.7, f32[21,128,128]{2,1,0:T(8,128)} %bitcast.4, s32[21]{0:T(128)} %reshape.20.refs_2_, f32[3,2,128,128]{3,2,1,0:T(8,128)} %bitcast.6, s32[6]{0:T(128)} %reshape.22.refs_4_), custom_call_target="tpu_custom_call" | custom-call | tf_op jit(solution)/shard_map/multigrid/pallas_call | solution.py:410
  97.4 1.6 %copy.9 = f32[1,1,3,128,128]{4,3,2,1,0:T(8,128)} copy(f32[1,1,3,128,128]{4,3,2,1,0:T(8,128)} %bitcast.5) | data formatting | bytes 393216

commit v2 on v0

v2 whole, which is shorter than its diff:
```python
import functools
import types

import jax
import jax.numpy as jnp
from jax import lax
from jax.experimental import pallas as pl
from jax.experimental.pallas import tpu as pltpu
from jax.sharding import PartitionSpec as P

B = 128
SLOTS = 3
OPT = 7
COEF_ZERO = 0.9
COEF_ONE = -0.36
COEF_TWO = 0.05
MESH = pl.DeviceIdType.MESH
F32 = jnp.float32
BF16 = jnp.bfloat16


def halves(value):
    high = value.astype(BF16)
    return high, (value - high.astype(F32)).astype(BF16)


def stacked(value):
    return jnp.concatenate(halves(value), axis=0)


def beside(value):
    return jnp.concatenate(halves(value), axis=1)


def product(left, right):
    full = jnp.dot(left, right, preferred_element_type=F32)
    rows, columns = full.shape[0] // 2, full.shape[1] // 2
    cross = full[:rows, columns:] + full[rows:, :columns]
    return full[:rows, :columns] + (cross + full[rows:, columns:])


def kernel(n_row, names, rhs_hbm, ops_hbm, cols, links_hbm, targets, out, *refs):
    m = types.SimpleNamespace(**dict(zip(names, refs)))
    lvl = lax.axis_index("lvl")
    row = lax.axis_index("row")
    is_fine = lvl < 5
    is_mid = (lvl >= 5) & (lvl < 7)
    is_coarse = lvl == 7
    plane = lvl < 4
    four = lvl == 4
    root = lvl == 0
    has = (row > 0, row < n_row - 1)
    near = (row - 1, row + 1)
    far = (-2, -1, 1, 2)
    has_far = (row > 1, row > 0, row < n_row - 1, row < n_row - 2)

    load_rhs = pltpu.make_async_copy(rhs_hbm, m.rhs, m.in_sem.at[0])
    load_links = pltpu.make_async_copy(links_hbm, m.links, m.in_sem.at[1])
    load_ops = pltpu.make_async_copy(ops_hbm, m.ops, m.in_sem.at[2])
    for load in (load_rhs, load_links, load_ops):
        load.start()

    barrier = pltpu.get_barrier_semaphore()
    for step in range(1, 8):
        pl.semaphore_signal(
            barrier, inc=1, device_id={"lvl": lax.rem(lvl + step, 8), "row": row}, device_id_type=MESH
        )
    for step, there in zip(far, has_far):
        @pl.when(there)
        def _():
            pl.semaphore_signal(
                barrier, inc=1, device_id={"lvl": lvl, "row": row + step}, device_id_type=MESH
            )

    def meet():
        pl.semaphore_wait(barrier, 7 + sum(one.astype(jnp.int32) for one in has_far))

    pending = []

    def go(make, cond=None):
        pending.append((make, cond))
        if cond is None:
            make().start()
        else:
            pl.when(cond)(lambda: make().start())

    def drain():
        for make, cond in pending:
            if cond is None:
                make().wait_send()
            else:
                pl.when(cond)(lambda: make().wait_send())
        pending.clear()

    def copy(src, dst, send, recv, to_lvl, to_row=None):
        return pltpu.make_async_remote_copy(
            src_ref=src, dst_ref=dst, send_sem=send, recv_sem=recv,
            device_id={"lvl": to_lvl, "row": row if to_row is None else to_row},
            device_id_type=MESH,
        )

    def arrived(ref, sem):
        pltpu.make_async_copy(ref, ref, sem).wait()

    def halo_go(turn, src, rows):
        part = pl.ds(0, rows)
        for side in range(2):
            go(
                lambda side=side: copy(
                    src.at[part], m.halo.at[turn, 1 - side, part],
                    m.halo_send.at[turn, side], m.halo_recv.at[turn, 1 - side], lvl, near[side],
                ),
                has[side],
            )

    def halo_arrived(turn, side, rows):
        arrived(m.halo.at[turn, side, pl.ds(0, rows)], m.halo_recv.at[turn, side])

    def code_of(s, j):
        return cols[s * OPT + j]

    def gathered_tile(s, code):
        total = jnp.zeros((B, B), F32)
        for j in range(OPT):
            total = total + jnp.where(code_of(s, j) == code, F32(1), F32(0)) * m.ops[s * OPT + j]
        return total

    def clear_missing(ref, conditions):
        for i, there in enumerate(conditions):
            @pl.when(jnp.logical_not(there))
            def _():
                ref[i] = jnp.zeros((B, B), F32)

    def coarse_send(cycle):
        for i in range(4):
            go(
                lambda i=i: copy(
                    m.cv.at[cycle], m.chalo.at[cycle, 3 - i],
                    m.chalo_send.at[cycle, i], m.chalo_recv.at[cycle, 3 - i], lvl, row + far[i],
                ),
                has_far[i] & (is_coarse if cycle == 0 else root),
            )

    def coarse_solve(cycle):
        own = product(m.st_own[...], beside(m.cv[cycle]))
        for i in range(4):
            @pl.when(has_far[i])
            def _():
                arrived(m.chalo.at[cycle, i], m.chalo_recv.at[cycle, i])
        around = beside(m.chalo[cycle].reshape(4 * B, B))
        m.fix[cycle] = own + product(m.st_far[...], around)

    def split_stencil():
        m.st_own[...] = stacked(m.st[2])
        for i, d in enumerate((0, 1, 3, 4)):
            m.st_far[:, pl.ds(i * B, B)] = stacked(m.st[d])

    @pl.when(is_fine)
    def _():
        load_links.wait()
        for s in range(SLOTS):
            for kind in range(2):
                m.link_parts[s, kind] = stacked(m.links[s, kind])
        load_rhs.wait()

        def restrict(cycle, resid_of):
            terms = [
                product(m.link_parts[s, 0], beside(resid_of(s))) for s in range(SLOTS)
            ]
            for k in range(4):
                total = jnp.zeros((B, B), F32)
                for s in range(SLOTS):
                    hit = jnp.where(targets[s * 2] == k, F32(1), F32(0))
                    total = total + hit * terms[s]
                m.rs_src[cycle, k] = total
            return terms

        def send_terms(cycle):
            for step in range(1, 4):
                to = lax.rem(lvl + step, 4)
                go(
                    lambda step=step, to=to: copy(
                        m.rs_src.at[cycle, to], m.rs_in.at[cycle, lvl],
                        m.rs_send.at[cycle, step], m.rs_recv.at[cycle, lvl], to,
                    ),
                    plane,
                )

        def plane_sum(cycle):
            total = m.rs_src[cycle, lvl]
            for step in range(1, 4):
                source = lax.rem(lvl + step, 4)
                arrived(m.rs_in.at[cycle, source], m.rs_recv.at[cycle, source])
                total = total + m.rs_in[cycle, source]
            return total

        def gather_go(cycle):
            for step in range(1, 4):
                go(
                    lambda step=step: copy(
                        m.fbuf.at[cycle, lvl], m.fbuf.at[cycle, lvl],
                        m.gather_send.at[cycle, step], m.f_recv.at[cycle, lvl], lax.rem(lvl + step, 4),
                    ),
                    plane,
                )

        def image(turn, src, dst):
            dst[...] = product(m.wide[1], beside(src[...]))
            for side in range(2):
                @pl.when(has[side])
                def _():
                    halo_arrived(turn, side, SLOTS * B)
                    dst[...] = dst[...] + product(m.wide[2 * side], beside(m.halo[turn, side]))

        def correct(cycle, dest):
            for s in range(SLOTS):
                chosen = m.fbuf[cycle, targets[s * 2 + 1]]
                rows = pl.ds(s * B, B)
                dest[rows] = m.smooth[rows] + product(m.link_parts[s, 1], beside(chosen))

        def blend(resid, first):
            return COEF_ZERO * resid[...] + COEF_ONE * first[...] + COEF_TWO * m.smooth[...]

        restrict(0, lambda s: m.rhs[pl.ds(s * B, B)])
        meet()
        send_terms(0)
        for k in range(4):
            go(
                lambda k=k: copy(
                    m.rs_src.at[0, k], m.mid_in.at[k % 2, 1],
                    m.four_send.at[k], m.mid_recv.at[k % 2, 1], 5 + k // 2,
                ),
                four,
            )
        halo_go(0, m.rhs, SLOTS * B)

        load_ops.wait()

        def dense(s, carry):
            for code in range(3 * SLOTS):
                high, low = halves(gathered_tile(s, code))
                columns = pl.ds((code % SLOTS) * B, B)
                m.wide[code // SLOTS, pl.ds(pl.multiple_of(s * B, B), B), columns] = high
                m.wide[code // SLOTS, pl.ds(pl.multiple_of((SLOTS + s) * B, B), B), columns] = low
            return carry

        lax.fori_loop(0, SLOTS, dense, 0)

        sum_copy = lambda: copy(
            m.sum_src, m.mid_in.at[lax.rem(lvl, 2), 0],
            m.sum_send, m.mid_recv.at[lax.rem(lvl, 2), 0], 5 + lvl // 2,
        )

        @pl.when(plane)
        def _():
            m.sum_src[...] = plane_sum(0)
            sum_copy().start()

        first = m.field.at[1]
        image(0, m.rhs, first)

        @pl.when(plane)
        def _():
            sum_copy().wait_send()

        halo_go(1, first, SLOTS * B)

        @pl.when(plane)
        def _():
            arrived(m.t_buf.at[lvl], m.t_recv.at[lvl])

        for step in range(1, 4):
            go(
                lambda step=step: copy(
                    m.t_buf.at[lvl], m.t_buf.at[lvl],
                    m.t_send.at[step], m.t_recv.at[lvl], lax.rem(lvl + step, 4),
                ),
                plane,
            )
        image(1, first, m.smooth)
        m.smooth[...] = blend(m.rhs, first)

        @pl.when(plane)
        def _():
            arrived(m.p_buf, m.p_recv)
            m.p_part[...] = stacked(m.p_buf[...])
            for step in range(1, 4):
                source = lax.rem(lvl + step, 4)
                arrived(m.t_buf.at[source], m.t_recv.at[source])

        @pl.when(four)
        def _():
            for k in range(4):
                arrived(m.t_buf.at[k], m.t_recv.at[k])

        for k in range(4):
            m.t_part[k] = stacked(m.t_buf[k])

        @pl.when(root)
        def _():
            arrived(m.st, m.st_recv)
            split_stencil()
            clear_missing(m.chalo.at[1], has_far)

        @pl.when(plane)
        def _():
            clear_missing(m.mhalo.at[0], has)
            clear_missing(m.mhalo.at[1], has)
            arrived(m.fbuf.at[0, lvl], m.f_recv.at[0, lvl])

        gather_go(0)

        @pl.when(plane)
        def _():
            for step in range(1, 4):
                source = lax.rem(lvl + step, 4)
                arrived(m.fbuf.at[0, source], m.f_recv.at[0, source])

        @pl.when(four)
        def _():
            for k in range(4):
                arrived(m.fbuf.at[0, k], m.f_recv.at[0, k])

        correct(0, m.sol)

        halo_go(2, m.sol, SLOTS * B)
        image(2, m.sol, m.smooth)
        resid = m.field.at[3]
        resid[...] = m.rhs[...] - m.smooth[...]
        terms = restrict(1, lambda s: m.field[3, pl.ds(s * B, B)])
        send_terms(1)
        for k in range(4):
            go(
                lambda k=k: copy(
                    m.rs_src.at[1, k], m.rs_in.at[1, 4], m.four_send.at[4 + k], m.rs_recv.at[1, 4], k
                ),
                four,
            )
        total = jnp.zeros((B, B), F32)
        for s in range(SLOTS):
            total = total + product(m.t_part[targets[s * 2]], beside(terms[s]))
        m.u_src[...] = total
        slot = jnp.maximum(lvl - 1, 0)
        go(
            lambda: copy(m.u_src, m.u_in.at[slot], m.u_send, m.u_recv.at[slot], 0),
            jnp.logical_not(root),
        )
        halo_go(3, resid, SLOTS * B)

        def mid_halo_go(turn):
            for side in range(2):
                go(
                    lambda side=side: copy(
                        m.mv.at[turn], m.mhalo.at[turn, 1 - side],
                        m.mhalo_send.at[turn, side], m.mhalo_recv.at[turn, 1 - side], lvl, near[side],
                    ),
                    has[side] & plane,
                )

        def mid_image(turn):
            own = product(m.small[0, 1], beside(m.mv[turn]))
            for side in range(2):
                @pl.when(has[side])
                def _():
                    arrived(m.mhalo.at[turn, side], m.mhalo_recv.at[turn, side])
            for side in range(2):
                own = own + product(m.small[0, 2 * side], beside(m.mhalo[turn, side]))
            return own

        @pl.when(plane)
        def _():
            total = plane_sum(1)
            arrived(m.rs_in.at[1, 4], m.rs_recv.at[1, 4])
            m.mv[0] = total + m.rs_in[1, 4]

        mid_halo_go(0)

        @pl.when(root)
        def _():
            total = m.u_src[...]
            for i in range(4):
                arrived(m.u_in.at[i], m.u_recv.at[i])
                total = total + m.u_in[i]
            m.cv[1] = total

        coarse_send(1)

        @pl.when(plane)
        def _():
            arrived(m.a_buf, m.a_recv)
            for d in range(3):
                m.small[0, d] = stacked(m.a_buf[d])

        first = m.field.at[4]
        image(3, resid, first)
        halo_go(4, first, SLOTS * B)

        @pl.when(plane)
        def _():
            m.mv[1] = mid_image(0)

        mid_halo_go(1)

        @pl.when(root)
        def _():
            coarse_solve(1)

        for to in (1, 2, 3, 7):
            go(
                lambda to=to: copy(
                    m.fix.at[1], m.fix.at[1], m.fix_send.at[1, to], m.fix_recv.at[1], to
                ),
                root,
            )

        @pl.when(plane)
        def _():
            m.mid_src[...] = COEF_ZERO * m.mv[0] + COEF_ONE * m.mv[1] + COEF_TWO * mid_image(1)

        @pl.when(plane & jnp.logical_not(root))
        def _():
            arrived(m.fix.at[1], m.fix_recv.at[1])

        @pl.when(plane)
        def _():
            value = m.mid_src[...] + product(m.p_part[...], beside(m.fix[1]))
            m.mid_src[...] = value
            m.fbuf[1, lvl] = value + m.fix[1]

        gather_go(1)
        go(
            lambda: copy(m.fbuf.at[1, lvl], m.fbuf.at[1, lvl], m.f_send.at[0, 0], m.f_recv.at[1, lvl], 4),
            plane,
        )
        go(
            lambda: copy(
                m.mid_src, m.mid_out.at[lax.rem(lvl, 2)], m.mid_send, m.mid_out_recv.at[lax.rem(lvl, 2)],
                5 + lvl // 2,
            ),
            plane,
        )
        image(4, first, m.smooth)
        m.smooth[...] = m.sol[...] + blend(resid, first)

        @pl.when(plane)
        def _():
            for step in range(1, 4):
                source = lax.rem(lvl + step, 4)
                arrived(m.fbuf.at[1, source], m.f_recv.at[1, source])

        @pl.when(four)
        def _():
            for k in range(4):
                arrived(m.fbuf.at[1, k], m.f_recv.at[1, k])

        correct(1, out)
        drain()

    @pl.when(is_mid)
    def _():
        pair = lvl - 5
        load_links.wait()
        eye = (
            lax.broadcasted_iota(jnp.int32, (B, B), 0) == lax.broadcasted_iota(jnp.int32, (B, B), 1)
        ).astype(F32)
        for p in range(2):
            tile = m.links[2 * p, 0] + 0.5 * eye
            m.t_src[p] = tile
            m.link_parts[2 * p, 0] = stacked(tile)
            m.link_parts[2 * p, 1] = stacked(m.links[2 * p, 1])
        load_rhs.wait()
        meet()
        for p in range(2):
            k = 2 * pair + p
            go(lambda p=p, k=k: copy(m.t_src.at[p], m.t_buf.at[k], m.t_send.at[p], m.t_recv.at[k], k))
            go(lambda p=p, k=k: copy(m.t_src.at[p], m.t_buf.at[k], m.t_send.at[2 + p], m.t_recv.at[k], 4))
        for p in range(2):
            k = 2 * pair + p
            go(lambda p=p, k=k: copy(m.links.at[2 * p, 1], m.p_buf, m.p_send.at[p], m.p_recv, k))
        load_ops.wait()
        for p in range(2):
            for d in range(3):
                tile = gathered_tile(2 * p, d * SLOTS + 2 * p)
                m.a_src[p, d] = tile
                m.small[p, d] = stacked(tile)

        def level_image(turn, dst):
            for p in range(2):
                part = pl.ds(p * B, B)
                dst[part] = product(m.small[p, 1], beside(m.field[turn, part]))
            for side in range(2):
                @pl.when(has[side])
                def _():
                    halo_arrived(turn, side, 2 * B)
                    for p in range(2):
                        part = pl.ds(p * B, B)
                        dst[part] = dst[part] + product(
                            m.small[p, 2 * side], beside(m.halo[turn, side, part])
                        )

        for p in range(2):
            for source in (1, 0):
                arrived(m.mid_in.at[p, source], m.mid_recv.at[p, source])
            m.field[0, pl.ds(p * B, B)] = m.mid_in[p, 0] + m.mid_in[p, 1]
        total = product(m.link_parts[0, 0], beside(m.field[0, pl.ds(0, B)]))
        m.part_src[...] = total + product(m.link_parts[2, 0], beside(m.field[0, pl.ds(B, B)]))
        go(lambda: copy(m.part_src, m.coarse_in.at[pair], m.part_send, m.coarse_recv.at[pair], 7))
        halo_go(0, m.field.at[0], 2 * B)
        level_image(0, m.field.at[1])
        halo_go(1, m.field.at[1], 2 * B)
        level_image(1, m.smooth)
        part = pl.ds(0, 2 * B)
        m.smooth[part] = (
            COEF_ZERO * m.field[0, part] + COEF_ONE * m.field[1, part] + COEF_TWO * m.smooth[part]
        )
        arrived(m.fix.at[0], m.fix_recv.at[0])
        coarse = beside(m.fix[0])
        for p in range(2):
            k = 2 * pair + p
            value = m.smooth[pl.ds(p * B, B)] + product(m.link_parts[2 * p, 1], coarse)
            m.fbuf[0, k] = value + m.fix[0]
            for way, to in enumerate((k, 4)):
                go(
                    lambda k=k, p=p, way=way, to=to: copy(
                        m.fbuf.at[0, k], m.fbuf.at[0, k], m.f_send.at[p, way], m.f_recv.at[0, k], to
                    )
                )
        for p in range(2):
            k = 2 * pair + p
            go(lambda p=p, k=k: copy(m.a_src.at[p], m.a_buf, m.a_send.at[p], m.a_recv, k))
        out[pl.ds(B, B)] = jnp.zeros((B, B), F32)
        for p in range(2):
            arrived(m.mid_out.at[p], m.mid_out_recv.at[p])
            out[pl.ds(2 * p * B, B)] = m.mid_out[p]
        drain()

    @pl.when(is_coarse)
    def _():
        load_links.wait()
        load_rhs.wait()
        load_ops.wait()
        for d in range(3):
            m.ac[d] = gathered_tile(1, d * SLOTS + 1)
        clear_missing(m.chalo.at[0], has_far)
        meet()
        for side in range(2):
            go(
                lambda side=side: copy(
                    m.ac, m.ahalo.at[1 - side], m.ahalo_send.at[side], m.ahalo_recv.at[1 - side], lvl, near[side]
                ),
                has[side],
            )
        eye = (
            lax.broadcasted_iota(jnp.int32, (B, B), 0) == lax.broadcasted_iota(jnp.int32, (B, B), 1)
        ).astype(F32)
        centre = stacked(m.ac[1])
        m.st[0] = jnp.zeros((B, B), F32)
        m.st[1] = COEF_ONE * m.ac[0] + COEF_TWO * product(centre, beside(m.ac[0]))
        m.st[2] = COEF_ZERO * eye + COEF_ONE * m.ac[1] + COEF_TWO * product(centre, beside(m.ac[1]))
        m.st[3] = COEF_ONE * m.ac[2] + COEF_TWO * product(centre, beside(m.ac[2]))
        m.st[4] = jnp.zeros((B, B), F32)
        for side in range(2):
            @pl.when(has[side])
            def _():
                arrived(m.ahalo.at[side], m.ahalo_recv.at[side])
                edge = stacked(m.ac[2 * side])
                for d in range(3):
                    to = 2 * side + d
                    m.st[to] = m.st[to] + COEF_TWO * product(edge, beside(m.ahalo[side, d]))
        split_stencil()
        for pair in range(2):
            arrived(m.coarse_in.at[pair], m.coarse_recv.at[pair])
        m.cv[0] = m.coarse_in[0] + m.coarse_in[1]
        coarse_send(0)
        coarse_solve(0)
        for pair in range(2):
            go(
                lambda pair=pair: copy(
                    m.fix.at[0], m.fix.at[0], m.fix_send.at[0, pair], m.fix_recv.at[0], 5 + pair
                )
            )
        go(lambda: copy(m.st, m.st, m.st_send, m.st_recv, 0))
        out[pl.ds(0, B)] = jnp.zeros((B, B), F32)
        out[pl.ds(2 * B, B)] = jnp.zeros((B, B), F32)
        arrived(m.fix.at[1], m.fix_recv.at[1])
        out[pl.ds(B, B)] = m.fix[1]
        drain()


def scratch():
    dma = lambda *shape: pltpu.SemaphoreType.DMA(shape)
    block = lambda *lead: pltpu.VMEM(lead + (B, B), F32)
    slab = lambda *lead: pltpu.VMEM(lead + (SLOTS * B, B), F32)
    parts = lambda *lead: pltpu.VMEM(lead + (2 * B, B), BF16)
    return dict(
        rhs=slab(), ops=block(SLOTS * OPT), links=block(SLOTS, 2),
        wide=pltpu.VMEM((3, 2 * SLOTS * B, SLOTS * B), BF16), small=parts(2, 3), link_parts=parts(SLOTS, 2),
        field=slab(5), halo=slab(5, 2), sol=slab(), smooth=slab(),
        rs_src=block(2, 4), rs_in=block(2, 5), sum_src=block(), mid_in=block(2, 2),
        part_src=block(), coarse_in=block(2), fix=block(2), fbuf=block(2, 4),
        t_src=block(2), t_buf=block(4), t_part=parts(4), p_buf=block(), p_part=parts(),
        a_src=block(2, 3), a_buf=block(3), ac=block(3), ahalo=block(2, 3),
        st=block(5), st_own=parts(), st_far=pltpu.VMEM((2 * B, 4 * B), BF16),
        cv=block(2), chalo=block(2, 4), u_src=block(), u_in=block(4),
        mv=block(2), mhalo=block(2, 2), mid_src=block(), mid_out=block(2),
        in_sem=dma(3), halo_send=dma(5, 2), halo_recv=dma(5, 2),
        rs_send=dma(2, 4), rs_recv=dma(2, 5), sum_send=pltpu.SemaphoreType.DMA, mid_recv=dma(2, 2),
        four_send=dma(8), part_send=pltpu.SemaphoreType.DMA, coarse_recv=dma(2),
        fix_send=dma(2, 8), fix_recv=dma(2), f_send=dma(2, 2), gather_send=dma(2, 4), f_recv=dma(2, 4),
        t_send=dma(4), t_recv=dma(4), p_send=dma(2), p_recv=pltpu.SemaphoreType.DMA,
        a_send=dma(2), a_recv=pltpu.SemaphoreType.DMA, ahalo_send=dma(2), ahalo_recv=dma(2),
        st_send=pltpu.SemaphoreType.DMA, st_recv=pltpu.SemaphoreType.DMA,
        chalo_send=dma(2, 4), chalo_recv=dma(2, 4), u_send=pltpu.SemaphoreType.DMA, u_recv=dma(4),
        mhalo_send=dma(2, 2), mhalo_recv=dma(2, 2), mid_send=pltpu.SemaphoreType.DMA, mid_out_recv=dma(2),
    )


def solution(mesh):
    n_row = mesh.shape["row"]

    def per_device(rhs, op_tiles, op_cols, link_tiles, level_links):
        held = scratch()
        out = pl.pallas_call(
            functools.partial(kernel, n_row, tuple(held)),
            name="multigrid",
            out_shape=jax.ShapeDtypeStruct((SLOTS * B, B), F32),
            in_specs=[
                pl.BlockSpec(memory_space=pl.ANY),
                pl.BlockSpec(memory_space=pl.ANY),
                pl.BlockSpec(memory_space=pltpu.SMEM),
                pl.BlockSpec(memory_space=pl.ANY),
                pl.BlockSpec(memory_space=pltpu.SMEM),
            ],
            out_specs=pl.BlockSpec(memory_space=pltpu.VMEM),
            scratch_shapes=list(held.values()),
            compiler_params=pltpu.CompilerParams(
                collective_id=0, has_side_effects=True, vmem_limit_bytes=60 * 1024 * 1024
            ),
        )(
            rhs.reshape(SLOTS * B, B),
            op_tiles.reshape(SLOTS * OPT, B, B),
            op_cols.reshape(SLOTS * OPT),
            link_tiles.reshape(SLOTS, 2, B, B),
            level_links.reshape(SLOTS * 2),
        )
        return out.reshape(1, 1, SLOTS, B, B)

    placed = (
        P("lvl", "row", None, None, None),
        P("lvl", "row", None, None, None, None),
        P("lvl", "row", None, None),
        P("lvl", "row", None, None, None, None),
        P("lvl", "row", None, None),
    )
    return jax.shard_map(
        per_device,
        mesh=mesh,
        in_specs=placed,
        out_specs=P("lvl", "row", None, None, None),
        check_vma=False,
    )
```

time: 863 us -> 101 us (0.12)
  the two profiles are of different devices: /device:TPU:8 before, /device:TPU:171 now
where the time goes in v2:
time: 101 us; the launch traced here: 100 us
  Pallas kernels  96 us (95%)
  local copies, waits for them, and re-layouts  3.63 us (4%)
    pallas_call x1, Pallas kernels, per_device(): pl.pallas_call(functools.partial(kernel, n_row, tuple(held)), name='multi...  96 us
    unnamed x2, local copies, waits for them, and re-layouts  2.38 us

profile of v2, /device:TPU:171, one launch (start us, length us, event | category | flops | bytes accessed | tf_op | source)
XLA Modules:
  0.0 100.3 jit_solution(10551557144077762764)
XLA Ops:
  0.0 0.7 reduce
  0.7 0.6 reshape.20.cols
  1.3 0.8 copy.7
  2.1 0.7 reshape.22.targets
  2.7 96.0 %multigrid.1 = f32[384,128]{1,0:T(8,128)} custom-call(f32[384,128]{1,0:T(8,128)} %bitcast.7, f32[21,128,128]{2,1,0:T(8,128)} %bitcast.4, s32[21]{0:T(128)} %reshape.20.cols, f32[3,2,128,128]{3,2,1,0:T(8,128)} %bitcast.6, s32[6]{0:T(128)} %reshape.22.targets), custom_call_target="tpu_custom_call" | custom-call | tf_op jit(solution)/shard_map/multigrid/pallas_call | solution.py:623
  98.7 1.6 %copy.9 = f32[1,1,3,128,128]{4,3,2,1,0:T(8,128)} copy(f32[1,1,3,128,128]{4,3,2,1,0:T(8,128)} %bitcast.5) | data formatting | bytes 393216

commit v3 on v2

--- a/solution.py
+++ b/solution.py
@@ -212,9 +212,14 @@
                     halo_arrived(turn, side, SLOTS * B)
                     dst[...] = dst[...] + product(m.wide[2 * side], beside(m.halo[turn, side]))
 
+        def raise_fix(cycle):
+            coarse = beside(m.fix[cycle])
+            for s in range(SLOTS):
+                m.lift[s] = m.fix[cycle] + product(m.p_part[targets[s * 2 + 1]], coarse)
+
         def correct(cycle, dest):
             for s in range(SLOTS):
-                chosen = m.fbuf[cycle, targets[s * 2 + 1]]
+                chosen = m.lift[s] + m.fbuf[cycle, targets[s * 2 + 1]]
                 rows = pl.ds(s * B, B)
                 dest[rows] = m.smooth[rows] + product(m.link_parts[s, 1], beside(chosen))
 
@@ -265,35 +270,46 @@
 
         halo_go(1, first, SLOTS * B)
 
-        @pl.when(plane)
-        def _():
-            arrived(m.t_buf.at[lvl], m.t_recv.at[lvl])
-
-        for step in range(1, 4):
-            go(
-                lambda step=step: copy(
-                    m.t_buf.at[lvl], m.t_buf.at[lvl],
-                    m.t_send.at[step], m.t_recv.at[lvl], lax.rem(lvl + step, 4),
-                ),
-                plane,
-            )
+        @pl.when(four)
+        def _():
+            arrived(m.t_buf.at[0], m.t_recv.at[0])
+            arrived(m.p_buf.at[0], m.p_recv.at[0])
+            arrived(m.a_buf, m.a_recv)
+
+        go(lambda: copy(m.p_buf.at[0], m.p_buf.at[0], m.hop_send.at[0], m.p_recv.at[0], 0), four)
+        go(lambda: copy(m.t_buf.at[0], m.t_buf.at[0], m.hop_send.at[1], m.t_recv.at[0], 0), four)
+        go(lambda: copy(m.a_buf, m.a_buf, m.hop_send.at[2], m.a_recv, 0), four)
         image(1, first, m.smooth)
         m.smooth[...] = blend(m.rhs, first)
 
-        @pl.when(plane)
-        def _():
-            arrived(m.p_buf, m.p_recv)
-            m.p_part[...] = stacked(m.p_buf[...])
+        for buf, send, recv in ((m.p_buf, m.p_send, m.p_recv), (m.t_buf, m.t_send, m.t_recv)):
+            @pl.when(plane)
+            def _():
+                arrived(buf.at[lvl], recv.at[lvl])
+
+            for step in range(1, 4):
+                go(
+                    lambda step=step, buf=buf, send=send, recv=recv: copy(
+                        buf.at[lvl], buf.at[lvl], send.at[step], recv.at[lvl], lax.rem(lvl + step, 4)
+                    ),
+                    plane,
+                )
+
+        @pl.when(plane)
+        def _():
             for step in range(1, 4):
                 source = lax.rem(lvl + step, 4)
+                arrived(m.p_buf.at[source], m.p_recv.at[source])
                 arrived(m.t_buf.at[source], m.t_recv.at[source])
 
         @pl.when(four)
         def _():
-            for k in range(4):
+            for k in range(1, 4):
+                arrived(m.p_buf.at[k], m.p_recv.at[k])
                 arrived(m.t_buf.at[k], m.t_recv.at[k])
 
         for k in range(4):
+            m.p_part[k] = stacked(m.p_buf[k])
             m.t_part[k] = stacked(m.t_buf[k])
 
         @pl.when(root)
@@ -310,6 +326,15 @@
 
         gather_go(0)
 
+        @pl.when(four)
+        def _():
+            arrived(m.fbuf.at[0, 0], m.f_recv.at[0, 0])
+
+        go(lambda: copy(m.fbuf.at[0, 0], m.fbuf.at[0, 0], m.hop_send.at[3], m.f_recv.at[0, 0], 0), four)
+        arrived(m.fix.at[0], m.fix_recv.at[0])
+        go(lambda: copy(m.fix.at[0], m.fix.at[0], m.hop_send.at[4], m.fix_recv.at[0], 0), four)
+        raise_fix(0)
+
         @pl.when(plane)
         def _():
             for step in range(1, 4):
@@ -318,7 +343,7 @@
 
         @pl.when(four)
         def _():
-            for k in range(4):
+            for k in range(1, 4):
                 arrived(m.fbuf.at[0, k], m.f_recv.at[0, k])
 
         correct(0, m.sol)
@@ -329,11 +354,9 @@
         resid[...] = m.rhs[...] - m.smooth[...]
         terms = restrict(1, lambda s: m.field[3, pl.ds(s * B, B)])
         send_terms(1)
-        for k in range(4):
+        for k in range(1, 4):
             go(
-                lambda k=k: copy(
-                    m.rs_src.at[1, k], m.rs_in.at[1, 4], m.four_send.at[4 + k], m.rs_recv.at[1, 4], k
-                ),
+                lambda k=k: copy(m.rs_src.at[1, k], m.hop_in, m.four_send.at[4 + k], m.hop_recv, 4 + k),
                 four,
             )
         total = jnp.zeros((B, B), F32)
@@ -344,6 +367,10 @@
         go(
             lambda: copy(m.u_src, m.u_in.at[slot], m.u_send, m.u_recv.at[slot], 0),
             jnp.logical_not(root),
+        )
+        go(
+            lambda: copy(m.rs_src.at[1, 0], m.rs_in.at[1, 4], m.four_send.at[4], m.rs_recv.at[1, 4], 0),
+            four,
         )
         halo_go(3, resid, SLOTS * B)
 
@@ -405,7 +432,7 @@
         def _():
             coarse_solve(1)
 
-        for to in (1, 2, 3, 7):
+        for to in (4, 2, 1, 3, 7):
             go(
                 lambda to=to: copy(
                     m.fix.at[1], m.fix.at[1], m.fix_send.at[1, to], m.fix_recv.at[1], to
@@ -415,23 +442,24 @@
 
         @pl.when(plane)
         def _():
-            m.mid_src[...] = COEF_ZERO * m.mv[0] + COEF_ONE * m.mv[1] + COEF_TWO * mid_image(1)
-
-        @pl.when(plane & jnp.logical_not(root))
-        def _():
-            arrived(m.fix.at[1], m.fix_recv.at[1])
-
-        @pl.when(plane)
-        def _():
-            value = m.mid_src[...] + product(m.p_part[...], beside(m.fix[1]))
-            m.mid_src[...] = value
-            m.fbuf[1, lvl] = value + m.fix[1]
+            m.fbuf[1, lvl] = COEF_ZERO * m.mv[0] + COEF_ONE * m.mv[1] + COEF_TWO * mid_image(1)
 
         gather_go(1)
         go(
             lambda: copy(m.fbuf.at[1, lvl], m.fbuf.at[1, lvl], m.f_send.at[0, 0], m.f_recv.at[1, lvl], 4),
             plane,
         )
+        image(4, first, m.smooth)
+        m.smooth[...] = m.sol[...] + blend(resid, first)
+
+        @pl.when(jnp.logical_not(root))
+        def _():
+            arrived(m.fix.at[1], m.fix_recv.at[1])
+
+        @pl.when(plane)
+        def _():
+            m.mid_src[...] = m.fbuf[1, lvl] + product(m.p_part[lvl], beside(m.fix[1]))
+
         go(
             lambda: copy(
                 m.mid_src, m.mid_out.at[lax.rem(lvl, 2)], m.mid_send, m.mid_out_recv.at[lax.rem(lvl, 2)],
@@ -439,8 +467,7 @@
             ),
             plane,
         )
-        image(4, first, m.smooth)
-        m.smooth[...] = m.sol[...] + blend(resid, first)
+        raise_fix(1)
 
         @pl.when(plane)
         def _():
@@ -455,6 +482,10 @@
 
         correct(1, out)
         drain()
+
+    def hop_up():
+        arrived(m.hop_in, m.hop_recv)
+        go(lambda: copy(m.hop_in, m.rs_in.at[1, 4], m.hop_send.at[1], m.rs_recv.at[1, 4], lvl - 4))
 
     @pl.when(is_mid)
     def _():
@@ -467,22 +498,26 @@
             tile = m.links[2 * p, 0] + 0.5 * eye
             m.t_src[p] = tile
             m.link_parts[2 * p, 0] = stacked(tile)
-            m.link_parts[2 * p, 1] = stacked(m.links[2 * p, 1])
         load_rhs.wait()
         meet()
+        def ship(src, dst, recv, send, k):
+            go(lambda: copy(src, dst, send.at[0], recv, 4))
+            go(lambda: copy(src, dst, send.at[1], recv, k + 4 * (k // 3)), k > 0)
+
         for p in range(2):
             k = 2 * pair + p
-            go(lambda p=p, k=k: copy(m.t_src.at[p], m.t_buf.at[k], m.t_send.at[p], m.t_recv.at[k], k))
-            go(lambda p=p, k=k: copy(m.t_src.at[p], m.t_buf.at[k], m.t_send.at[2 + p], m.t_recv.at[k], 4))
-        for p in range(2):
-            k = 2 * pair + p
-            go(lambda p=p, k=k: copy(m.links.at[2 * p, 1], m.p_buf, m.p_send.at[p], m.p_recv, k))
+            ship(m.links.at[2 * p, 1], m.p_buf.at[k], m.p_recv.at[k], m.p_send.at[pl.ds(2 * p, 2)], k)
+            ship(m.t_src.at[p], m.t_buf.at[k], m.t_recv.at[k], m.t_send.at[pl.ds(2 * p, 2)], k)
         load_ops.wait()
         for p in range(2):
             for d in range(3):
                 tile = gathered_tile(2 * p, d * SLOTS + 2 * p)
                 m.a_src[p, d] = tile
                 m.small[p, d] = stacked(tile)
+        for p in range(2):
+            k = 2 * pair + p
+            to = k + 4 * (1 - (lax.rem(k, 3) + 1) // 2)
+            go(lambda p=p, to=to: copy(m.a_src.at[p], m.a_buf, m.a_send.at[p], m.a_recv, to))
 
         def level_image(turn, dst):
             for p in range(2):
@@ -513,21 +548,13 @@
         m.smooth[part] = (
             COEF_ZERO * m.field[0, part] + COEF_ONE * m.field[1, part] + COEF_TWO * m.smooth[part]
         )
-        arrived(m.fix.at[0], m.fix_recv.at[0])
-        coarse = beside(m.fix[0])
         for p in range(2):
             k = 2 * pair + p
-            value = m.smooth[pl.ds(p * B, B)] + product(m.link_parts[2 * p, 1], coarse)
-            m.fbuf[0, k] = value + m.fix[0]
-            for way, to in enumerate((k, 4)):
-                go(
-                    lambda k=k, p=p, way=way, to=to: copy(
-                        m.fbuf.at[0, k], m.fbuf.at[0, k], m.f_send.at[p, way], m.f_recv.at[0, k], to
-                    )
-                )
-        for p in range(2):
-            k = 2 * pair + p
-            go(lambda p=p, k=k: copy(m.a_src.at[p], m.a_buf, m.a_send.at[p], m.a_recv, k))
+            m.fbuf[0, k] = m.smooth[pl.ds(p * B, B)]
+            ship(m.fbuf.at[0, k], m.fbuf.at[0, k], m.f_recv.at[0, k], m.f_send.at[p], k)
+        arrived(m.fix.at[0], m.fix_recv.at[0])
+        go(lambda: copy(m.fix.at[0], m.fix.at[0], m.hop_send.at[0], m.fix_recv.at[0], lvl - 4))
+        hop_up()
         out[pl.ds(B, B)] = jnp.zeros((B, B), F32)
         for p in range(2):
             arrived(m.mid_out.at[p], m.mid_out_recv.at[p])
@@ -567,19 +594,28 @@
                 for d in range(3):
                     to = 2 * side + d
                     m.st[to] = m.st[to] + COEF_TWO * product(edge, beside(m.ahalo[side, d]))
+        go(lambda: copy(m.st, m.st, m.st_send, m.st_recv, 0))
         split_stencil()
+        arrived(m.p_buf.at[3], m.p_recv.at[3])
+        go(lambda: copy(m.p_buf.at[3], m.p_buf.at[3], m.p_send.at[0], m.p_recv.at[3], 3))
+        arrived(m.t_buf.at[3], m.t_recv.at[3])
+        go(lambda: copy(m.t_buf.at[3], m.t_buf.at[3], m.t_send.at[0], m.t_recv.at[3], 3))
+        arrived(m.a_buf, m.a_recv)
+        go(lambda: copy(m.a_buf, m.a_buf, m.a_send.at[0], m.a_recv, 3))
         for pair in range(2):
             arrived(m.coarse_in.at[pair], m.coarse_recv.at[pair])
         m.cv[0] = m.coarse_in[0] + m.coarse_in[1]
         coarse_send(0)
         coarse_solve(0)
-        for pair in range(2):
+        for to in (5, 4, 6, 3):
             go(
-                lambda pair=pair: copy(
-                    m.fix.at[0], m.fix.at[0], m.fix_send.at[0, pair], m.fix_recv.at[0], 5 + pair
+                lambda to=to: copy(
+                    m.fix.at[0], m.fix.at[0], m.fix_send.at[0, to], m.fix_recv.at[0], to
                 )
             )
-        go(lambda: copy(m.st, m.st, m.st_send, m.st_recv, 0))
+        arrived(m.fbuf.at[0, 3], m.f_recv.at[0, 3])
+        go(lambda: copy(m.fbuf.at[0, 3], m.fbuf.at[0, 3], m.f_send.at[0, 0], m.f_recv.at[0, 3], 3))
+        hop_up()
         out[pl.ds(0, B)] = jnp.zeros((B, B), F32)
         out[pl.ds(2 * B, B)] = jnp.zeros((B, B), F32)
         arrived(m.fix.at[1], m.fix_recv.at[1])
@@ -598,7 +634,7 @@
         field=slab(5), halo=slab(5, 2), sol=slab(), smooth=slab(),
         rs_src=block(2, 4), rs_in=block(2, 5), sum_src=block(), mid_in=block(2, 2),
         part_src=block(), coarse_in=block(2), fix=block(2), fbuf=block(2, 4),
-        t_src=block(2), t_buf=block(4), t_part=parts(4), p_buf=block(), p_part=parts(),
+        t_src=block(2), t_buf=block(4), t_part=parts(4), p_buf=block(4), p_part=parts(4), lift=block(SLOTS), hop_in=block(),
         a_src=block(2, 3), a_buf=block(3), ac=block(3), ahalo=block(2, 3),
         st=block(5), st_own=parts(), st_far=pltpu.VMEM((2 * B, 4 * B), BF16),
         cv=block(2), chalo=block(2, 4), u_src=block(), u_in=block(4),
@@ -607,7 +643,7 @@
         rs_send=dma(2, 4), rs_recv=dma(2, 5), sum_send=pltpu.SemaphoreType.DMA, mid_recv=dma(2, 2),
         four_send=dma(8), part_send=pltpu.SemaphoreType.DMA, coarse_recv=dma(2),
         fix_send=dma(2, 8), fix_recv=dma(2), f_send=dma(2, 2), gather_send=dma(2, 4), f_recv=dma(2, 4),
-        t_send=dma(4), t_recv=dma(4), p_send=dma(2), p_recv=pltpu.SemaphoreType.DMA,
+        t_send=dma(4), t_recv=dma(4), p_send=dma(4), p_recv=dma(4), hop_send=dma(5), hop_recv=pltpu.SemaphoreType.DMA,
         a_send=dma(2), a_recv=pltpu.SemaphoreType.DMA, ahalo_send=dma(2), ahalo_recv=dma(2),
         st_send=pltpu.SemaphoreType.DMA, st_recv=pltpu.SemaphoreType.DMA,
         chalo_send=dma(2, 4), chalo_recv=dma(2, 4), u_send=pltpu.SemaphoreType.DMA, u_recv=dma(4),

time: 101 us -> 102 us (level)
  the two profiles are of different devices: /device:TPU:171 before, /device:TPU:506 now
where the time goes in v3:
time: 102 us
  Pallas kernels  97.9 us (96%)
  local copies, waits for them, and re-layouts  3.63 us (4%)
    pallas_call x1, Pallas kernels, per_device(): pl.pallas_call(functools.partial(kernel, n_row, tuple(held)), name='multi...  97.9 us
    unnamed x2, local copies, waits for them, and re-layouts  2.38 us

profile of v3, /device:TPU:506, one launch (start us, length us, event | category | flops | bytes accessed | tf_op | source)
XLA Modules:
  0.0 102.2 jit_solution(5221914833148998614)
XLA Ops:
  0.0 0.7 reduce
  0.7 0.6 reshape.20.cols
  1.3 0.8 copy.7
  2.1 0.7 reshape.22.targets
  2.7 97.9 %multigrid.1 = f32[384,128]{1,0:T(8,128)} custom-call(f32[384,128]{1,0:T(8,128)} %bitcast.7, f32[21,128,128]{2,1,0:T(8,128)} %bitcast.4, s32[21]{0:T(128)} %reshape.20.cols, f32[3,2,128,128]{3,2,1,0:T(8,128)} %bitcast.6, s32[6]{0:T(128)} %reshape.22.targets), custom_call_target="tpu_custom_call" | custom-call | tf_op jit(solution)/shard_map/multigrid/pallas_call | solution.py:659
  100.6 1.6 %copy.9 = f32[1,1,3,128,128]{4,3,2,1,0:T(8,128)} copy(f32[1,1,3,128,128]{4,3,2,1,0:T(8,128)} %bitcast.5) | data formatting | bytes 393216

commit v4 on v3

--- a/solution.py
+++ b/solution.py
@@ -117,7 +117,7 @@
         arrived(m.halo.at[turn, side, pl.ds(0, rows)], m.halo_recv.at[turn, side])
 
     def code_of(s, j):
-        return cols[s * OPT + j]
+        return cols[0, 0, s, j]
 
     def gathered_tile(s, code):
         total = jnp.zeros((B, B), F32)
@@ -131,29 +131,25 @@
             def _():
                 ref[i] = jnp.zeros((B, B), F32)
 
-    def coarse_send(cycle):
-        for i in range(4):
+    def side_go(turn, src, halo, send, recv, cond):
+        for side in range(2):
             go(
-                lambda i=i: copy(
-                    m.cv.at[cycle], m.chalo.at[cycle, 3 - i],
-                    m.chalo_send.at[cycle, i], m.chalo_recv.at[cycle, 3 - i], lvl, row + far[i],
+                lambda side=side: copy(
+                    src.at[turn], halo.at[turn, 1 - side],
+                    send.at[turn, side], recv.at[turn, 1 - side], lvl, near[side],
                 ),
-                has_far[i] & (is_coarse if cycle == 0 else root),
-            )
-
-    def coarse_solve(cycle):
-        own = product(m.st_own[...], beside(m.cv[cycle]))
-        for i in range(4):
-            @pl.when(has_far[i])
+                has[side] & cond,
+            )
+
+    def side_image(turn, parts, src, halo, recv):
+        own = product(parts(1), beside(src[turn]))
+        for side in range(2):
+            @pl.when(has[side])
             def _():
-                arrived(m.chalo.at[cycle, i], m.chalo_recv.at[cycle, i])
-        around = beside(m.chalo[cycle].reshape(4 * B, B))
-        m.fix[cycle] = own + product(m.st_far[...], around)
-
-    def split_stencil():
-        m.st_own[...] = stacked(m.st[2])
-        for i, d in enumerate((0, 1, 3, 4)):
-            m.st_far[:, pl.ds(i * B, B)] = stacked(m.st[d])
+                arrived(halo.at[turn, side], recv.at[turn, side])
+        for side in range(2):
+            own = own + product(parts(2 * side), beside(halo[turn, side]))
+        return own
 
     @pl.when(is_fine)
     def _():
@@ -170,7 +166,7 @@
             for k in range(4):
                 total = jnp.zeros((B, B), F32)
                 for s in range(SLOTS):
-                    hit = jnp.where(targets[s * 2] == k, F32(1), F32(0))
+                    hit = jnp.where(targets[0, 0, s, 0] == k, F32(1), F32(0))
                     total = total + hit * terms[s]
                 m.rs_src[cycle, k] = total
             return terms
@@ -215,11 +211,11 @@
         def raise_fix(cycle):
             coarse = beside(m.fix[cycle])
             for s in range(SLOTS):
-                m.lift[s] = m.fix[cycle] + product(m.p_part[targets[s * 2 + 1]], coarse)
+                m.lift[s] = m.fix[cycle] + product(m.p_part[targets[0, 0, s, 1]], coarse)
 
         def correct(cycle, dest):
             for s in range(SLOTS):
-                chosen = m.lift[s] + m.fbuf[cycle, targets[s * 2 + 1]]
+                chosen = m.lift[s] + m.fbuf[cycle, targets[0, 0, s, 1]]
                 rows = pl.ds(s * B, B)
                 dest[rows] = m.smooth[rows] + product(m.link_parts[s, 1], beside(chosen))
 
@@ -268,69 +264,66 @@
         def _():
             sum_copy().wait_send()
 
-        halo_go(1, first, SLOTS * B)
-
         @pl.when(four)
         def _():
+            arrived(m.p_buf.at[0], m.p_recv.at[0])
             arrived(m.t_buf.at[0], m.t_recv.at[0])
-            arrived(m.p_buf.at[0], m.p_recv.at[0])
-            arrived(m.a_buf, m.a_recv)
 
         go(lambda: copy(m.p_buf.at[0], m.p_buf.at[0], m.hop_send.at[0], m.p_recv.at[0], 0), four)
         go(lambda: copy(m.t_buf.at[0], m.t_buf.at[0], m.hop_send.at[1], m.t_recv.at[0], 0), four)
-        go(lambda: copy(m.a_buf, m.a_buf, m.hop_send.at[2], m.a_recv, 0), four)
+        halo_go(1, first, SLOTS * B)
         image(1, first, m.smooth)
         m.smooth[...] = blend(m.rhs, first)
 
-        for buf, send, recv in ((m.p_buf, m.p_send, m.p_recv), (m.t_buf, m.t_send, m.t_recv)):
+        def spread_tile(buf, send, recv):
             @pl.when(plane)
             def _():
                 arrived(buf.at[lvl], recv.at[lvl])
 
             for step in range(1, 4):
                 go(
-                    lambda step=step, buf=buf, send=send, recv=recv: copy(
+                    lambda step=step: copy(
                         buf.at[lvl], buf.at[lvl], send.at[step], recv.at[lvl], lax.rem(lvl + step, 4)
                     ),
                     plane,
                 )
 
+        spread_tile(m.p_buf, m.p_send, m.p_recv)
+
+        @pl.when(four)
+        def _():
+            arrived(m.a_buf, m.a_recv)
+
+        go(lambda: copy(m.a_buf, m.a_buf, m.hop_send.at[2], m.a_recv, 0), four)
+
+        @pl.when(root)
+        def _():
+            clear_missing(m.khalo.at[0], has)
+            clear_missing(m.khalo.at[1], has)
+
+        @pl.when(plane)
+        def _():
+            clear_missing(m.mhalo.at[0], has)
+            clear_missing(m.mhalo.at[1], has)
+            arrived(m.fbuf.at[0, lvl], m.f_recv.at[0, lvl])
+
+        gather_go(0)
+        spread_tile(m.t_buf, m.t_send, m.t_recv)
+
         @pl.when(plane)
         def _():
             for step in range(1, 4):
                 source = lax.rem(lvl + step, 4)
                 arrived(m.p_buf.at[source], m.p_recv.at[source])
-                arrived(m.t_buf.at[source], m.t_recv.at[source])
 
         @pl.when(four)
         def _():
             for k in range(1, 4):
                 arrived(m.p_buf.at[k], m.p_recv.at[k])
-                arrived(m.t_buf.at[k], m.t_recv.at[k])
 
         for k in range(4):
             m.p_part[k] = stacked(m.p_buf[k])
-            m.t_part[k] = stacked(m.t_buf[k])
-
-        @pl.when(root)
-        def _():
-            arrived(m.st, m.st_recv)
-            split_stencil()
-            clear_missing(m.chalo.at[1], has_far)
-
-        @pl.when(plane)
-        def _():
-            clear_missing(m.mhalo.at[0], has)
-            clear_missing(m.mhalo.at[1], has)
-            arrived(m.fbuf.at[0, lvl], m.f_recv.at[0, lvl])
-
-        gather_go(0)
-
-        @pl.when(four)
-        def _():
-            arrived(m.fbuf.at[0, 0], m.f_recv.at[0, 0])
-
-        go(lambda: copy(m.fbuf.at[0, 0], m.fbuf.at[0, 0], m.hop_send.at[3], m.f_recv.at[0, 0], 0), four)
+
         arrived(m.fix.at[0], m.fix_recv.at[0])
         go(lambda: copy(m.fix.at[0], m.fix.at[0], m.hop_send.at[4], m.fix_recv.at[0], 0), four)
         raise_fix(0)
@@ -343,12 +336,27 @@
 
         @pl.when(four)
         def _():
+            for k in range(4):
+                arrived(m.fbuf.at[0, k], m.f_recv.at[0, k])
+
+        correct(0, m.sol)
+
+        halo_go(2, m.sol, SLOTS * B)
+
+        @pl.when(plane)
+        def _():
+            for step in range(1, 4):
+                source = lax.rem(lvl + step, 4)
+                arrived(m.t_buf.at[source], m.t_recv.at[source])
+
+        @pl.when(four)
+        def _():
             for k in range(1, 4):
-                arrived(m.fbuf.at[0, k], m.f_recv.at[0, k])
-
-        correct(0, m.sol)
-
-        halo_go(2, m.sol, SLOTS * B)
+                arrived(m.t_buf.at[k], m.t_recv.at[k])
+
+        for k in range(4):
+            m.t_part[k] = stacked(m.t_buf[k])
+
         image(2, m.sol, m.smooth)
         resid = m.field.at[3]
         resid[...] = m.rhs[...] - m.smooth[...]
@@ -361,7 +369,7 @@
             )
         total = jnp.zeros((B, B), F32)
         for s in range(SLOTS):
-            total = total + product(m.t_part[targets[s * 2]], beside(terms[s]))
+            total = total + product(m.t_part[targets[0, 0, s, 0]], beside(terms[s]))
         m.u_src[...] = total
         slot = jnp.maximum(lvl - 1, 0)
         go(
@@ -374,25 +382,14 @@
         )
         halo_go(3, resid, SLOTS * B)
 
-        def mid_halo_go(turn):
-            for side in range(2):
-                go(
-                    lambda side=side: copy(
-                        m.mv.at[turn], m.mhalo.at[turn, 1 - side],
-                        m.mhalo_send.at[turn, side], m.mhalo_recv.at[turn, 1 - side], lvl, near[side],
-                    ),
-                    has[side] & plane,
-                )
+        mid_sides = (m.mv, m.mhalo, m.mhalo_send, m.mhalo_recv)
+        top_sides = (m.kv, m.khalo, m.khalo_send, m.khalo_recv)
 
         def mid_image(turn):
-            own = product(m.small[0, 1], beside(m.mv[turn]))
-            for side in range(2):
-                @pl.when(has[side])
-                def _():
-                    arrived(m.mhalo.at[turn, side], m.mhalo_recv.at[turn, side])
-            for side in range(2):
-                own = own + product(m.small[0, 2 * side], beside(m.mhalo[turn, side]))
-            return own
+            return side_image(turn, lambda d: m.small[0, d], m.mv, m.mhalo, m.mhalo_recv)
+
+        def top_image(turn):
+            return side_image(turn, lambda d: m.small[1, d], m.kv, m.khalo, m.khalo_recv)
 
         @pl.when(plane)
         def _():
@@ -400,7 +397,7 @@
             arrived(m.rs_in.at[1, 4], m.rs_recv.at[1, 4])
             m.mv[0] = total + m.rs_in[1, 4]
 
-        mid_halo_go(0)
+        side_go(0, *mid_sides, plane)
 
         @pl.when(root)
         def _():
@@ -408,9 +405,9 @@
             for i in range(4):
                 arrived(m.u_in.at[i], m.u_recv.at[i])
                 total = total + m.u_in[i]
-            m.cv[1] = total
-
-        coarse_send(1)
+            m.kv[0] = total
+
+        side_go(0, *top_sides, root)
 
         @pl.when(plane)
         def _():
@@ -418,21 +415,33 @@
             for d in range(3):
                 m.small[0, d] = stacked(m.a_buf[d])
 
+        @pl.when(root)
+        def _():
+            arrived(m.ac, m.ac_recv)
+            for d in range(3):
+                m.small[1, d] = stacked(m.ac[d])
+
         first = m.field.at[4]
         image(3, resid, first)
+
+        @pl.when(plane)
+        def _():
+            m.mv[1] = mid_image(0)
+
+        side_go(1, *mid_sides, plane)
+
+        @pl.when(root)
+        def _():
+            m.kv[1] = top_image(0)
+
+        side_go(1, *top_sides, root)
         halo_go(4, first, SLOTS * B)
 
-        @pl.when(plane)
-        def _():
-            m.mv[1] = mid_image(0)
-
-        mid_halo_go(1)
-
         @pl.when(root)
         def _():
-            coarse_solve(1)
-
-        for to in (4, 2, 1, 3, 7):
+            m.fix[1] = COEF_ZERO * m.kv[0] + COEF_ONE * m.kv[1] + COEF_TWO * top_image(1)
+
+        for to in (4, 2, 1, 3):
             go(
                 lambda to=to: copy(
                     m.fix.at[1], m.fix.at[1], m.fix_send.at[1, to], m.fix_recv.at[1], to
@@ -449,6 +458,13 @@
             lambda: copy(m.fbuf.at[1, lvl], m.fbuf.at[1, lvl], m.f_send.at[0, 0], m.f_recv.at[1, lvl], 4),
             plane,
         )
+        go(
+            lambda: copy(
+                m.fbuf.at[1, lvl], m.mid_out.at[lax.rem(lvl, 2)], m.mid_send, m.mid_out_recv.at[lax.rem(lvl, 2)],
+                5 + lvl // 2,
+            ),
+            plane & jnp.logical_not(root),
+        )
         image(4, first, m.smooth)
         m.smooth[...] = m.sol[...] + blend(resid, first)
 
@@ -456,16 +472,9 @@
         def _():
             arrived(m.fix.at[1], m.fix_recv.at[1])
 
-        @pl.when(plane)
-        def _():
-            m.mid_src[...] = m.fbuf[1, lvl] + product(m.p_part[lvl], beside(m.fix[1]))
-
         go(
-            lambda: copy(
-                m.mid_src, m.mid_out.at[lax.rem(lvl, 2)], m.mid_send, m.mid_out_recv.at[lax.rem(lvl, 2)],
-                5 + lvl // 2,
-            ),
-            plane,
+            lambda: copy(m.fix.at[1], m.fix.at[1], m.fix_send.at[1, 5], m.fix_recv.at[1], lvl + 4),
+            plane & jnp.logical_not(root),
         )
         raise_fix(1)
 
@@ -477,7 +486,13 @@
 
         @pl.when(four)
         def _():
-            for k in range(4):
+            arrived(m.fbuf.at[1, 0], m.f_recv.at[1, 0])
+
+        go(lambda: copy(m.fbuf.at[1, 0], m.mid_out.at[0], m.mid_send, m.mid_out_recv.at[0], 5), four)
+
+        @pl.when(four)
+        def _():
+            for k in range(1, 4):
                 arrived(m.fbuf.at[1, k], m.f_recv.at[1, k])
 
         correct(1, out)
@@ -498,8 +513,13 @@
             tile = m.links[2 * p, 0] + 0.5 * eye
             m.t_src[p] = tile
             m.link_parts[2 * p, 0] = stacked(tile)
+            m.link_parts[2 * p, 1] = stacked(m.links[2 * p, 1])
         load_rhs.wait()
         meet()
+        def smooth_go(p, way, to):
+            k = 2 * pair + p
+            go(lambda: copy(m.fbuf.at[0, k], m.fbuf.at[0, k], m.f_send.at[p, way], m.f_recv.at[0, k], to))
+
         def ship(src, dst, recv, send, k):
             go(lambda: copy(src, dst, send.at[0], recv, 4))
             go(lambda: copy(src, dst, send.at[1], recv, k + 4 * (k // 3)), k > 0)
@@ -551,14 +571,19 @@
         for p in range(2):
             k = 2 * pair + p
             m.fbuf[0, k] = m.smooth[pl.ds(p * B, B)]
-            ship(m.fbuf.at[0, k], m.fbuf.at[0, k], m.f_recv.at[0, k], m.f_send.at[p], k)
+            smooth_go(p, 0, k)
         arrived(m.fix.at[0], m.fix_recv.at[0])
         go(lambda: copy(m.fix.at[0], m.fix.at[0], m.hop_send.at[0], m.fix_recv.at[0], lvl - 4))
+        for p in range(2):
+            smooth_go(p, 1, 4)
         hop_up()
         out[pl.ds(B, B)] = jnp.zeros((B, B), F32)
+        arrived(m.fix.at[1], m.fix_recv.at[1])
+        for p in range(2):
+            m.lift[p] = product(m.link_parts[2 * p, 1], beside(m.fix[1]))
         for p in range(2):
             arrived(m.mid_out.at[p], m.mid_out_recv.at[p])
-            out[pl.ds(2 * p * B, B)] = m.mid_out[p]
+            out[pl.ds(2 * p * B, B)] = m.mid_out[p] + m.lift[p]
         drain()
 
     @pl.when(is_coarse)
@@ -568,7 +593,7 @@
         load_ops.wait()
         for d in range(3):
             m.ac[d] = gathered_tile(1, d * SLOTS + 1)
-        clear_missing(m.chalo.at[0], has_far)
+        clear_missing(m.chalo, has_far)
         meet()
         for side in range(2):
             go(
@@ -577,6 +602,7 @@
                 ),
                 has[side],
             )
+        go(lambda: copy(m.ac, m.ac, m.st_send, m.ac_recv, 0))
         eye = (
             lax.broadcasted_iota(jnp.int32, (B, B), 0) == lax.broadcasted_iota(jnp.int32, (B, B), 1)
         ).astype(F32)
@@ -594,27 +620,37 @@
                 for d in range(3):
                     to = 2 * side + d
                     m.st[to] = m.st[to] + COEF_TWO * product(edge, beside(m.ahalo[side, d]))
-        go(lambda: copy(m.st, m.st, m.st_send, m.st_recv, 0))
-        split_stencil()
+        st_own = stacked(m.st[2])
+        for i, d in enumerate((0, 1, 3, 4)):
+            m.st_far[:, pl.ds(i * B, B)] = stacked(m.st[d])
         arrived(m.p_buf.at[3], m.p_recv.at[3])
         go(lambda: copy(m.p_buf.at[3], m.p_buf.at[3], m.p_send.at[0], m.p_recv.at[3], 3))
-        arrived(m.t_buf.at[3], m.t_recv.at[3])
-        go(lambda: copy(m.t_buf.at[3], m.t_buf.at[3], m.t_send.at[0], m.t_recv.at[3], 3))
-        arrived(m.a_buf, m.a_recv)
-        go(lambda: copy(m.a_buf, m.a_buf, m.a_send.at[0], m.a_recv, 3))
         for pair in range(2):
             arrived(m.coarse_in.at[pair], m.coarse_recv.at[pair])
-        m.cv[0] = m.coarse_in[0] + m.coarse_in[1]
-        coarse_send(0)
-        coarse_solve(0)
+        m.cv[...] = m.coarse_in[0] + m.coarse_in[1]
+        for i in range(4):
+            go(
+                lambda i=i: copy(
+                    m.cv, m.chalo.at[3 - i], m.chalo_send.at[i], m.chalo_recv.at[3 - i], lvl, row + far[i]
+                ),
+                has_far[i],
+            )
+        own = product(st_own, beside(m.cv[...]))
+        for i in range(4):
+            @pl.when(has_far[i])
+            def _():
+                arrived(m.chalo.at[i], m.chalo_recv.at[i])
+        m.fix[0] = own + product(m.st_far[...], beside(m.chalo[...].reshape(4 * B, B)))
         for to in (5, 4, 6, 3):
             go(
                 lambda to=to: copy(
                     m.fix.at[0], m.fix.at[0], m.fix_send.at[0, to], m.fix_recv.at[0], to
                 )
             )
-        arrived(m.fbuf.at[0, 3], m.f_recv.at[0, 3])
-        go(lambda: copy(m.fbuf.at[0, 3], m.fbuf.at[0, 3], m.f_send.at[0, 0], m.f_recv.at[0, 3], 3))
+        arrived(m.t_buf.at[3], m.t_recv.at[3])
+        go(lambda: copy(m.t_buf.at[3], m.t_buf.at[3], m.t_send.at[0], m.t_recv.at[3], 3))
+        arrived(m.a_buf, m.a_recv)
+        go(lambda: copy(m.a_buf, m.a_buf, m.a_send.at[0], m.a_recv, 3))
         hop_up()
         out[pl.ds(0, B)] = jnp.zeros((B, B), F32)
         out[pl.ds(2 * B, B)] = jnp.zeros((B, B), F32)
@@ -636,17 +672,17 @@
         part_src=block(), coarse_in=block(2), fix=block(2), fbuf=block(2, 4),
         t_src=block(2), t_buf=block(4), t_part=parts(4), p_buf=block(4), p_part=parts(4), lift=block(SLOTS), hop_in=block(),
         a_src=block(2, 3), a_buf=block(3), ac=block(3), ahalo=block(2, 3),
-        st=block(5), st_own=parts(), st_far=pltpu.VMEM((2 * B, 4 * B), BF16),
-        cv=block(2), chalo=block(2, 4), u_src=block(), u_in=block(4),
-        mv=block(2), mhalo=block(2, 2), mid_src=block(), mid_out=block(2),
+        st=block(5), st_far=pltpu.VMEM((2 * B, 4 * B), BF16),
+        cv=block(), chalo=block(4), kv=block(2), khalo=block(2, 2), u_src=block(), u_in=block(4),
+        mv=block(2), mhalo=block(2, 2), mid_out=block(2),
         in_sem=dma(3), halo_send=dma(5, 2), halo_recv=dma(5, 2),
         rs_send=dma(2, 4), rs_recv=dma(2, 5), sum_send=pltpu.SemaphoreType.DMA, mid_recv=dma(2, 2),
         four_send=dma(8), part_send=pltpu.SemaphoreType.DMA, coarse_recv=dma(2),
         fix_send=dma(2, 8), fix_recv=dma(2), f_send=dma(2, 2), gather_send=dma(2, 4), f_recv=dma(2, 4),
         t_send=dma(4), t_recv=dma(4), p_send=dma(4), p_recv=dma(4), hop_send=dma(5), hop_recv=pltpu.SemaphoreType.DMA,
         a_send=dma(2), a_recv=pltpu.SemaphoreType.DMA, ahalo_send=dma(2), ahalo_recv=dma(2),
-        st_send=pltpu.SemaphoreType.DMA, st_recv=pltpu.SemaphoreType.DMA,
-        chalo_send=dma(2, 4), chalo_recv=dma(2, 4), u_send=pltpu.SemaphoreType.DMA, u_recv=dma(4),
+        st_send=pltpu.SemaphoreType.DMA, ac_recv=pltpu.SemaphoreType.DMA,
+        chalo_send=dma(4), chalo_recv=dma(4), khalo_send=dma(2, 2), khalo_recv=dma(2, 2), u_send=pltpu.SemaphoreType.DMA, u_recv=dma(4),
         mhalo_send=dma(2, 2), mhalo_recv=dma(2, 2), mid_send=pltpu.SemaphoreType.DMA, mid_out_recv=dma(2),
     )
 
@@ -675,9 +711,9 @@
         )(
             rhs.reshape(SLOTS * B, B),
             op_tiles.reshape(SLOTS * OPT, B, B),
-            op_cols.reshape(SLOTS * OPT),
+            op_cols,
             link_tiles.reshape(SLOTS, 2, B, B),
-            level_links.reshape(SLOTS * 2),
+            level_links,
         )
         return out.reshape(1, 1, SLOTS, B, B)
 

time: 102 us -> 90.7 us (0.89)
  the two profiles are of different devices: /device:TPU:506 before, /device:TPU:362 now
where the time goes in v4:
time: 90.7 us; the launch traced here: 90.4 us
  Pallas kernels  86.2 us (95%)
  local copies, waits for them, and re-layouts  4.21 us (5%)
    pallas_call x1, Pallas kernels, per_device(): pl.pallas_call(functools.partial(kernel, n_row, tuple(held)), name='multi...  86.2 us
    unnamed x3, local copies, waits for them, and re-layouts  4.21 us

profile of v4, /device:TPU:362, one launch (start us, length us, event | category | flops | bytes accessed | tf_op | source)
XLA Modules:
  0.0 90.4 jit_solution(4389681417206981938)
XLA Ops:
  0.0 1.3 %copy.6.cols = s32[1,1,3,7]{3,2,1,0:T(4,128)} copy(s32[1,1,3,7]{3,1,2,0:T(1,128)} %param.7) | data formatting | bytes 168 | tf_op args[2]
  1.3 1.3 %copy.7.targets = s32[1,1,3,2]{3,2,1,0:T(4,128)} copy(s32[1,1,3,2]{2,3,1,0:T(2,128)} %param.9) | data formatting | bytes 48 | tf_op args[4]
  2.6 86.2 %multigrid.1 = f32[384,128]{1,0:T(8,128)} custom-call(f32[384,128]{1,0:T(8,128)} %bitcast.7, f32[21,128,128]{2,1,0:T(8,128)} %bitcast.4, s32[1,1,3,7]{3,2,1,0:T(4,128)} %copy.6.cols, f32[3,2,128,128]{3,2,1,0:T(8,128)} %bitcast.6, s32[1,1,3,2]{3,2,1,0:T(4,128)} %copy.7.targets), custom_call_target="tpu_custom_call" | custom-call | tf_op jit(solution)/shard_map/multigrid/pallas_call | solution.py:695
  88.8 1.6 %copy.9 = f32[1,1,3,128,128]{4,3,2,1,0:T(8,128)} copy(f32[1,1,3,128,128]{4,3,2,1,0:T(8,128)} %bitcast.5) | data formatting | bytes 393216

commit v5 on v4

--- a/solution.py
+++ b/solution.py
@@ -117,7 +117,7 @@
         arrived(m.halo.at[turn, side, pl.ds(0, rows)], m.halo_recv.at[turn, side])
 
     def code_of(s, j):
-        return cols[0, 0, s, j]
+        return cols[0, s, 0, j]
 
     def gathered_tile(s, code):
         total = jnp.zeros((B, B), F32)
@@ -166,7 +166,7 @@
             for k in range(4):
                 total = jnp.zeros((B, B), F32)
                 for s in range(SLOTS):
-                    hit = jnp.where(targets[0, 0, s, 0] == k, F32(1), F32(0))
+                    hit = jnp.where(targets[0, 0, 0, s] == k, F32(1), F32(0))
                     total = total + hit * terms[s]
                 m.rs_src[cycle, k] = total
             return terms
@@ -211,11 +211,11 @@
         def raise_fix(cycle):
             coarse = beside(m.fix[cycle])
             for s in range(SLOTS):
-                m.lift[s] = m.fix[cycle] + product(m.p_part[targets[0, 0, s, 1]], coarse)
+                m.lift[s] = m.fix[cycle] + product(m.p_part[targets[0, 0, 1, s]], coarse)
 
         def correct(cycle, dest):
             for s in range(SLOTS):
-                chosen = m.lift[s] + m.fbuf[cycle, targets[0, 0, s, 1]]
+                chosen = m.lift[s] + m.fbuf[cycle, targets[0, 0, 1, s]]
                 rows = pl.ds(s * B, B)
                 dest[rows] = m.smooth[rows] + product(m.link_parts[s, 1], beside(chosen))
 
@@ -267,10 +267,8 @@
         @pl.when(four)
         def _():
             arrived(m.p_buf.at[0], m.p_recv.at[0])
-            arrived(m.t_buf.at[0], m.t_recv.at[0])
 
         go(lambda: copy(m.p_buf.at[0], m.p_buf.at[0], m.hop_send.at[0], m.p_recv.at[0], 0), four)
-        go(lambda: copy(m.t_buf.at[0], m.t_buf.at[0], m.hop_send.at[1], m.t_recv.at[0], 0), four)
         halo_go(1, first, SLOTS * B)
         image(1, first, m.smooth)
         m.smooth[...] = blend(m.rhs, first)
@@ -308,7 +306,6 @@
             arrived(m.fbuf.at[0, lvl], m.f_recv.at[0, lvl])
 
         gather_go(0)
-        spread_tile(m.t_buf, m.t_send, m.t_recv)
 
         @pl.when(plane)
         def _():
@@ -327,6 +324,7 @@
         arrived(m.fix.at[0], m.fix_recv.at[0])
         go(lambda: copy(m.fix.at[0], m.fix.at[0], m.hop_send.at[4], m.fix_recv.at[0], 0), four)
         raise_fix(0)
+        spread_tile(m.t_buf, m.t_send, m.t_recv)
 
         @pl.when(plane)
         def _():
@@ -342,20 +340,6 @@
         correct(0, m.sol)
 
         halo_go(2, m.sol, SLOTS * B)
-
-        @pl.when(plane)
-        def _():
-            for step in range(1, 4):
-                source = lax.rem(lvl + step, 4)
-                arrived(m.t_buf.at[source], m.t_recv.at[source])
-
-        @pl.when(four)
-        def _():
-            for k in range(1, 4):
-                arrived(m.t_buf.at[k], m.t_recv.at[k])
-
-        for k in range(4):
-            m.t_part[k] = stacked(m.t_buf[k])
 
         image(2, m.sol, m.smooth)
         resid = m.field.at[3]
@@ -367,9 +351,23 @@
                 lambda k=k: copy(m.rs_src.at[1, k], m.hop_in, m.four_send.at[4 + k], m.hop_recv, 4 + k),
                 four,
             )
+        @pl.when(plane)
+        def _():
+            for step in range(1, 4):
+                source = lax.rem(lvl + step, 4)
+                arrived(m.t_buf.at[source], m.t_recv.at[source])
+
+        @pl.when(four)
+        def _():
+            for k in range(4):
+                arrived(m.t_buf.at[k], m.t_recv.at[k])
+
+        for k in range(4):
+            m.t_part[k] = stacked(m.t_buf[k])
+
         total = jnp.zeros((B, B), F32)
         for s in range(SLOTS):
-            total = total + product(m.t_part[targets[0, 0, s, 0]], beside(terms[s]))
+            total = total + product(m.t_part[targets[0, 0, 0, s]], beside(terms[s]))
         m.u_src[...] = total
         slot = jnp.maximum(lvl - 1, 0)
         go(
@@ -436,18 +434,6 @@
 
         side_go(1, *top_sides, root)
         halo_go(4, first, SLOTS * B)
-
-        @pl.when(root)
-        def _():
-            m.fix[1] = COEF_ZERO * m.kv[0] + COEF_ONE * m.kv[1] + COEF_TWO * top_image(1)
-
-        for to in (4, 2, 1, 3):
-            go(
-                lambda to=to: copy(
-                    m.fix.at[1], m.fix.at[1], m.fix_send.at[1, to], m.fix_recv.at[1], to
-                ),
-                root,
-            )
 
         @pl.when(plane)
         def _():
@@ -465,8 +451,26 @@
             ),
             plane & jnp.logical_not(root),
         )
+        @pl.when(root)
+        def _():
+            m.fix[1] = COEF_ZERO * m.kv[0] + COEF_ONE * m.kv[1] + COEF_TWO * top_image(1)
+
+        for to in (4, 2, 1, 3):
+            go(
+                lambda to=to: copy(
+                    m.fix.at[1], m.fix.at[1], m.fix_send.at[1, to], m.fix_recv.at[1], to
+                ),
+                root,
+            )
+
         image(4, first, m.smooth)
         m.smooth[...] = m.sol[...] + blend(resid, first)
+
+        @pl.when(four)
+        def _():
+            arrived(m.fbuf.at[1, 0], m.f_recv.at[1, 0])
+
+        go(lambda: copy(m.fbuf.at[1, 0], m.mid_out.at[0], m.mid_send, m.mid_out_recv.at[0], 5), four)
 
         @pl.when(jnp.logical_not(root))
         def _():
@@ -483,12 +487,6 @@
             for step in range(1, 4):
                 source = lax.rem(lvl + step, 4)
                 arrived(m.fbuf.at[1, source], m.f_recv.at[1, source])
-
-        @pl.when(four)
-        def _():
-            arrived(m.fbuf.at[1, 0], m.f_recv.at[1, 0])
-
-        go(lambda: copy(m.fbuf.at[1, 0], m.mid_out.at[0], m.mid_send, m.mid_out_recv.at[0], 5), four)
 
         @pl.when(four)
         def _():
@@ -522,12 +520,11 @@
 
         def ship(src, dst, recv, send, k):
             go(lambda: copy(src, dst, send.at[0], recv, 4))
-            go(lambda: copy(src, dst, send.at[1], recv, k + 4 * (k // 3)), k > 0)
+            go(lambda: copy(src, dst, send.at[1], recv, k), k > 0)
 
         for p in range(2):
             k = 2 * pair + p
             ship(m.links.at[2 * p, 1], m.p_buf.at[k], m.p_recv.at[k], m.p_send.at[pl.ds(2 * p, 2)], k)
-            ship(m.t_src.at[p], m.t_buf.at[k], m.t_recv.at[k], m.t_send.at[pl.ds(2 * p, 2)], k)
         load_ops.wait()
         for p in range(2):
             for d in range(3):
@@ -538,6 +535,13 @@
             k = 2 * pair + p
             to = k + 4 * (1 - (lax.rem(k, 3) + 1) // 2)
             go(lambda p=p, to=to: copy(m.a_src.at[p], m.a_buf, m.a_send.at[p], m.a_recv, to))
+        for p in range(2):
+            k = 2 * pair + p
+            go(
+                lambda p=p, k=k: copy(
+                    m.t_src.at[p], m.t_buf.at[k], m.t_send.at[p], m.t_recv.at[k], k
+                )
+            )
 
         def level_image(turn, dst):
             for p in range(2):
@@ -572,10 +576,13 @@
             k = 2 * pair + p
             m.fbuf[0, k] = m.smooth[pl.ds(p * B, B)]
             smooth_go(p, 0, k)
+        for p in range(2):
+            smooth_go(p, 1, 4)
         arrived(m.fix.at[0], m.fix_recv.at[0])
         go(lambda: copy(m.fix.at[0], m.fix.at[0], m.hop_send.at[0], m.fix_recv.at[0], lvl - 4))
         for p in range(2):
-            smooth_go(p, 1, 4)
+            k = 2 * pair + p
+            go(lambda p=p, k=k: copy(m.t_src.at[p], m.t_buf.at[k], m.t_send.at[2 + p], m.t_recv.at[k], 4))
         hop_up()
         out[pl.ds(B, B)] = jnp.zeros((B, B), F32)
         arrived(m.fix.at[1], m.fix_recv.at[1])
@@ -623,8 +630,6 @@
         st_own = stacked(m.st[2])
         for i, d in enumerate((0, 1, 3, 4)):
             m.st_far[:, pl.ds(i * B, B)] = stacked(m.st[d])
-        arrived(m.p_buf.at[3], m.p_recv.at[3])
-        go(lambda: copy(m.p_buf.at[3], m.p_buf.at[3], m.p_send.at[0], m.p_recv.at[3], 3))
         for pair in range(2):
             arrived(m.coarse_in.at[pair], m.coarse_recv.at[pair])
         m.cv[...] = m.coarse_in[0] + m.coarse_in[1]
@@ -647,8 +652,6 @@
                     m.fix.at[0], m.fix.at[0], m.fix_send.at[0, to], m.fix_recv.at[0], to
                 )
             )
-        arrived(m.t_buf.at[3], m.t_recv.at[3])
-        go(lambda: copy(m.t_buf.at[3], m.t_buf.at[3], m.t_send.at[0], m.t_recv.at[3], 3))
         arrived(m.a_buf, m.a_recv)
         go(lambda: copy(m.a_buf, m.a_buf, m.a_send.at[0], m.a_recv, 3))
         hop_up()
@@ -711,9 +714,9 @@
         )(
             rhs.reshape(SLOTS * B, B),
             op_tiles.reshape(SLOTS * OPT, B, B),
-            op_cols,
+            op_cols.transpose(0, 2, 1, 3),
             link_tiles.reshape(SLOTS, 2, B, B),
-            level_links,
+            level_links.transpose(0, 1, 3, 2),
         )
         return out.reshape(1, 1, SLOTS, B, B)
 

time: 90.7 us -> 87.9 us (0.969)
  the two profiles are of different devices: /device:TPU:362 before, /device:TPU:124 now
where the time goes in v5:
time: 87.9 us; the launch traced here: 87.7 us
  Pallas kernels  86.1 us (98%)
  local copies, waits for them, and re-layouts  1.62 us (2%)
    pallas_call x1, Pallas kernels, per_device(): pl.pallas_call(functools.partial(kernel, n_row, tuple(held)), name='multi...  86.1 us

profile of v5, /device:TPU:124, one launch (start us, length us, event | category | flops | bytes accessed | tf_op | source)
XLA Modules:
  0.0 87.7 jit_solution(14741701092456306960)
XLA Ops:
  0.0 86.1 %multigrid.1 = f32[384,128]{1,0:T(8,128)} custom-call(f32[384,128]{1,0:T(8,128)} %bitcast.9, f32[21,128,128]{2,1,0:T(8,128)} %bitcast.6, s32[1,3,1,7]{3,2,1,0:T(1,128)} %bitcast.10, f32[3,2,128,128]{3,2,1,0:T(8,128)} %bitcast.8, s32[1,1,2,3]{3,2,1,0:T(2,128)} %bitcast.11), custom_call_target="tpu_custom_call" | custom-call | tf_op jit(solution)/shard_map/multigrid/pallas_call | solution.py:698
  86.1 1.6 %copy.7 = f32[1,1,3,128,128]{4,3,2,1,0:T(8,128)} copy(f32[1,1,3,128,128]{4,3,2,1,0:T(8,128)} %bitcast.7) | data formatting | bytes 393216

commit v6 on v5

--- a/solution.py
+++ b/solution.py
@@ -102,7 +102,16 @@
     def arrived(ref, sem):
         pltpu.make_async_copy(ref, ref, sem).wait()
 
-    def halo_go(turn, src, rows):
+    def out_copy(src, slot):
+        return pltpu.make_async_copy(src, out.at[pl.ds(slot * B, B)], m.out_sem.at[slot])
+
+    def store(src, slot):
+        out_copy(src, slot).start()
+
+    def stored(slot):
+        out_copy(m.res.at[pl.ds(slot * B, B)], slot).wait()
+
+    def halo_go(turn, src, rows, cond=True):
         part = pl.ds(0, rows)
         for side in range(2):
             go(
@@ -110,7 +119,7 @@
                     src.at[part], m.halo.at[turn, 1 - side, part],
                     m.halo_send.at[turn, side], m.halo_recv.at[turn, 1 - side], lvl, near[side],
                 ),
-                has[side],
+                has[side] & cond,
             )
 
     def halo_arrived(turn, side, rows):
@@ -218,6 +227,8 @@
                 chosen = m.lift[s] + m.fbuf[cycle, targets[0, 0, 1, s]]
                 rows = pl.ds(s * B, B)
                 dest[rows] = m.smooth[rows] + product(m.link_parts[s, 1], beside(chosen))
+                if cycle == 1:
+                    store(dest.at[rows], s)
 
         def blend(resid, first):
             return COEF_ZERO * resid[...] + COEF_ONE * first[...] + COEF_TWO * m.smooth[...]
@@ -344,6 +355,7 @@
         image(2, m.sol, m.smooth)
         resid = m.field.at[3]
         resid[...] = m.rhs[...] - m.smooth[...]
+        halo_go(3, resid, SLOTS * B, plane)
         terms = restrict(1, lambda s: m.field[3, pl.ds(s * B, B)])
         send_terms(1)
         for k in range(1, 4):
@@ -378,7 +390,7 @@
             lambda: copy(m.rs_src.at[1, 0], m.rs_in.at[1, 4], m.four_send.at[4], m.rs_recv.at[1, 4], 0),
             four,
         )
-        halo_go(3, resid, SLOTS * B)
+        halo_go(3, resid, SLOTS * B, four)
 
         mid_sides = (m.mv, m.mhalo, m.mhalo_send, m.mhalo_recv)
         top_sides = (m.kv, m.khalo, m.khalo_send, m.khalo_recv)
@@ -493,8 +505,10 @@
             for k in range(1, 4):
                 arrived(m.fbuf.at[1, k], m.f_recv.at[1, k])
 
-        correct(1, out)
+        correct(1, m.res)
         drain()
+        for slot in range(SLOTS):
+            stored(slot)
 
     def hop_up():
         arrived(m.hop_in, m.hop_recv)
@@ -503,6 +517,8 @@
     @pl.when(is_mid)
     def _():
         pair = lvl - 5
+        m.res[pl.ds(B, B)] = jnp.zeros((B, B), F32)
+        store(m.res.at[pl.ds(B, B)], 1)
         load_links.wait()
         eye = (
             lax.broadcasted_iota(jnp.int32, (B, B), 0) == lax.broadcasted_iota(jnp.int32, (B, B), 1)
@@ -584,17 +600,23 @@
             k = 2 * pair + p
             go(lambda p=p, k=k: copy(m.t_src.at[p], m.t_buf.at[k], m.t_send.at[2 + p], m.t_recv.at[k], 4))
         hop_up()
-        out[pl.ds(B, B)] = jnp.zeros((B, B), F32)
         arrived(m.fix.at[1], m.fix_recv.at[1])
         for p in range(2):
             m.lift[p] = product(m.link_parts[2 * p, 1], beside(m.fix[1]))
         for p in range(2):
             arrived(m.mid_out.at[p], m.mid_out_recv.at[p])
-            out[pl.ds(2 * p * B, B)] = m.mid_out[p] + m.lift[p]
+            rows = pl.ds(2 * p * B, B)
+            m.res[rows] = m.mid_out[p] + m.lift[p]
+            store(m.res.at[rows], 2 * p)
         drain()
+        for slot in range(SLOTS):
+            stored(slot)
 
     @pl.when(is_coarse)
     def _():
+        m.res[...] = jnp.zeros((SLOTS * B, B), F32)
+        for slot in (0, 2):
+            store(m.res.at[pl.ds(slot * B, B)], slot)
         load_links.wait()
         load_rhs.wait()
         load_ops.wait()
@@ -655,11 +677,11 @@
         arrived(m.a_buf, m.a_recv)
         go(lambda: copy(m.a_buf, m.a_buf, m.a_send.at[0], m.a_recv, 3))
         hop_up()
-        out[pl.ds(0, B)] = jnp.zeros((B, B), F32)
-        out[pl.ds(2 * B, B)] = jnp.zeros((B, B), F32)
         arrived(m.fix.at[1], m.fix_recv.at[1])
-        out[pl.ds(B, B)] = m.fix[1]
+        store(m.fix.at[1], 1)
         drain()
+        for slot in range(SLOTS):
+            stored(slot)
 
 
 def scratch():
@@ -673,12 +695,12 @@
         field=slab(5), halo=slab(5, 2), sol=slab(), smooth=slab(),
         rs_src=block(2, 4), rs_in=block(2, 5), sum_src=block(), mid_in=block(2, 2),
         part_src=block(), coarse_in=block(2), fix=block(2), fbuf=block(2, 4),
-        t_src=block(2), t_buf=block(4), t_part=parts(4), p_buf=block(4), p_part=parts(4), lift=block(SLOTS), hop_in=block(),
+        t_src=block(2), t_buf=block(4), t_part=parts(4), p_buf=block(4), p_part=parts(4), lift=block(SLOTS), hop_in=block(), res=slab(),
         a_src=block(2, 3), a_buf=block(3), ac=block(3), ahalo=block(2, 3),
         st=block(5), st_far=pltpu.VMEM((2 * B, 4 * B), BF16),
         cv=block(), chalo=block(4), kv=block(2), khalo=block(2, 2), u_src=block(), u_in=block(4),
         mv=block(2), mhalo=block(2, 2), mid_out=block(2),
-        in_sem=dma(3), halo_send=dma(5, 2), halo_recv=dma(5, 2),
+        in_sem=dma(3), out_sem=dma(SLOTS), halo_send=dma(5, 2), halo_recv=dma(5, 2),
         rs_send=dma(2, 4), rs_recv=dma(2, 5), sum_send=pltpu.SemaphoreType.DMA, mid_recv=dma(2, 2),
         four_send=dma(8), part_send=pltpu.SemaphoreType.DMA, coarse_recv=dma(2),
         fix_send=dma(2, 8), fix_recv=dma(2), f_send=dma(2, 2), gather_send=dma(2, 4), f_recv=dma(2, 4),
@@ -706,7 +728,7 @@
                 pl.BlockSpec(memory_space=pl.ANY),
                 pl.BlockSpec(memory_space=pltpu.SMEM),
             ],
-            out_specs=pl.BlockSpec(memory_space=pltpu.VMEM),
+            out_specs=pl.BlockSpec(memory_space=pl.ANY),
             scratch_shapes=list(held.values()),
             compiler_params=pltpu.CompilerParams(
                 collective_id=0, has_side_effects=True, vmem_limit_bytes=60 * 1024 * 1024

time: 87.9 us -> 87.5 us (level)
  the two profiles are of different devices: /device:TPU:124 before, /device:TPU:314 now
where the time goes in v6:
time: 87.5 us; the launch traced here: 87.4 us
  Pallas kernels  85.7 us (98%)
  local copies, waits for them, and re-layouts  1.62 us (2%)
    pallas_call x1, Pallas kernels, per_device(): pl.pallas_call(functools.partial(kernel, n_row, tuple(held)), name='multi...  85.7 us

profile of v6, /device:TPU:314, one launch (start us, length us, event | category | flops | bytes accessed | tf_op | source)
XLA Modules:
  0.0 87.4 jit_solution(6694144003086667127)
XLA Ops:
  0.0 85.7 %multigrid.1 = f32[384,128]{1,0:T(8,128)} custom-call(f32[384,128]{1,0:T(8,128)} %bitcast.9, f32[21,128,128]{2,1,0:T(8,128)} %bitcast.6, s32[1,3,1,7]{3,2,1,0:T(1,128)} %bitcast.10, f32[3,2,128,128]{3,2,1,0:T(8,128)} %bitcast.8, s32[1,1,2,3]{3,2,1,0:T(2,128)} %bitcast.11), custom_call_target="tpu_custom_call" | custom-call | tf_op jit(solution)/shard_map/multigrid/pallas_call | solution.py:720
  85.7 1.6 %copy.7 = f32[1,1,3,128,128]{4,3,2,1,0:T(8,128)} copy(f32[1,1,3,128,128]{4,3,2,1,0:T(8,128)} %bitcast.7) | data formatting | bytes 393216

commit v7 on v6

--- a/solution.py
+++ b/solution.py
@@ -591,7 +591,9 @@
         for p in range(2):
             k = 2 * pair + p
             m.fbuf[0, k] = m.smooth[pl.ds(p * B, B)]
-            smooth_go(p, 0, k)
+        for q in range(2):
+            p = lax.rem(q + pair, 2)
+            smooth_go(p, 0, 2 * pair + p)
         for p in range(2):
             smooth_go(p, 1, 4)
         arrived(m.fix.at[0], m.fix_recv.at[0])

time: 87.5 us -> 88.1 us (level)
  the two profiles are of different devices: /device:TPU:314 before, /device:TPU:124 now
where the time goes in v7:
time: 88.1 us; the launch traced here: 87.9 us
  Pallas kernels  86.3 us (98%)
  local copies, waits for them, and re-layouts  1.62 us (2%)
    pallas_call x1, Pallas kernels, per_device(): pl.pallas_call(functools.partial(kernel, n_row, tuple(held)), name='multi...  86.3 us

profile of v7, /device:TPU:124, one launch (start us, length us, event | category | flops | bytes accessed | tf_op | source)
XLA Modules:
  0.0 87.9 jit_solution(11184383306161421368)
XLA Ops:
  0.0 86.3 %multigrid.1 = f32[384,128]{1,0:T(8,128)} custom-call(f32[384,128]{1,0:T(8,128)} %bitcast.9, f32[21,128,128]{2,1,0:T(8,128)} %bitcast.6, s32[1,3,1,7]{3,2,1,0:T(1,128)} %bitcast.10, f32[3,2,128,128]{3,2,1,0:T(8,128)} %bitcast.8, s32[1,1,2,3]{3,2,1,0:T(2,128)} %bitcast.11), custom_call_target="tpu_custom_call" | custom-call | tf_op jit(solution)/shard_map/multigrid/pallas_call | solution.py:722
  86.3 1.6 %copy.7 = f32[1,1,3,128,128]{4,3,2,1,0:T(8,128)} copy(f32[1,1,3,128,128]{4,3,2,1,0:T(8,128)} %bitcast.7) | data formatting | bytes 393216
